TPU v7x, 32 devices: a whole 2x2x4 slice. The times are simulated.
32 devices in a mesh: row: 4 (over x, core), col: 8 (over z, y).
Axes of the slice: x: 2, y: 2, z: 4, core: 2. Of those that a mesh axis runs over, the one named last changes fastest.
Arguments:
- masters: float32 [128, 4096], P('col'), may hold values from -6 to 6
- inst_master: int32 [64, 128], P('row', 'col'), may hold values from 0 to 127
- inst_orient: int32 [64, 128], P('row', 'col'), may hold values from 0 to 3
- owner_map: int32 [128], replicated, may hold values from 0 to 127, each once
- tile_free: float32 [4096, 8192], P('row', 'col'), may hold values from -3 to 3
- target: float32 [4096, 8192], P('row', 'col'), may hold values from 0 to 1
- kernel_spectra: float32 [2, 128, 8, 128], replicated, may hold values from -6 to 6
- socs_weights: float32 [8], replicated, may hold values from 0.05 to 1
Outputs:
- resist: float32 [4096, 8192], P('row', 'col')
- new_mask: float32 [4096, 8192], P('row', 'col')
- masters_out: float32 [128, 4096], P('col')
Inputs may be any that keep to these rules, and one draw needn't show every extreme that they name: `inst_orient`: bit 0 reverses a cell's rows, bit 1 its columns. `owner_map`: each storage row is used by exactly one master; storage row r lies on index r // 16 of col.
All inputs are finite; a program needn't handle non-finite values.
Results may differ from a plain program's by a relative error of at most 0.0092.
Values may be sent and summed in bfloat16 or wider, within the bound.
A program may use at most 128 MiB of HBM per device.

v0:
```python
import functools
import math

import jax
import jax.numpy as jnp
import numpy as np
from jax import lax
from jax.experimental import pallas as pl
from jax.experimental.pallas import tpu as pltpu
from jax.sharding import PartitionSpec as P

TILE = 512
TPD = 2
HALO = 64
CELL = 64
LANES = 128
HALF = CELL // 2
BLOCK = 512

step_free = 1.0
step_master = 0.05
resist_gain = 2.0
resist_level = 1.8


def dot(left, right):
    return jnp.dot(left, right, preferred_element_type=jnp.float32)


def tables(pad_side, band_side, halo, tile):
    freqs = np.arange(band_side, dtype=np.int64) - band_side // 2
    phases = (freqs[:, None] * np.arange(pad_side)[None, :]) % pad_side
    angles = phases.astype(np.float32) * np.float32(2.0 * math.pi / pad_side)
    cos = np.cos(angles)
    sin = np.sin(angles)
    cos_in = cos[:, halo : halo + tile]
    sin_in = sin[:, halo : halo + tile]
    cs_full = np.concatenate([cos, sin], 0)
    cs_lanes = np.pad(cs_full, ((0, 0), (LANES - halo, LANES - halo)))
    cs_in = np.concatenate([cos_in, sin_in], 0)
    field = np.block([[cos_in, sin_in], [-sin_in, cos_in]])
    parts = (cs_full, cs_lanes.T, cs_in, cs_in.T, field, field.T)
    return [jnp.asarray(np.ascontiguousarray(p).astype(jnp.bfloat16)) for p in parts]


def placements():
    rows_place = np.zeros((4, CELL, 2 * CELL), np.float32)
    cols_place = np.zeros((4, LANES, LANES), np.float32)
    for f in range(4):
        for side in range(2):
            flip = (f >> side) & 1
            for r in range(HALF):
                for h in range(2):
                    y = 2 * r + h
                    rows_place[f, CELL - 1 - y if flip else y, side * CELL + h * HALF + r] = 1
            for x in range(CELL):
                cols_place[f, side * CELL + x, side * CELL + (CELL - 1 - x if flip else x)] = 1
    cast = lambda v: jnp.asarray(np.ascontiguousarray(v).astype(jnp.bfloat16))
    return cast(rows_place), cast(rows_place.transpose(0, 2, 1)), cast(cols_place)


def left_mask(rows):
    return lax.broadcasted_iota(jnp.int32, (rows, LANES), 1) < CELL


def pair_codes(inst_ref, orient_ref, owner_ref, a, b):
    s0 = owner_ref[inst_ref[a, b]]
    s1 = owner_ref[inst_ref[a, b + 1]]
    o0 = orient_ref[a, b]
    o1 = orient_ref[a, b + 1]
    return s0, s1, (o0 & 1) + 2 * (o1 & 1), (o0 >> 1) + 2 * (o1 >> 1)


def assemble_pair(table_ref, rows_ref, cols_ref, codes):
    s0, s1, fr, fc = codes
    left = left_mask(HALF)
    p0 = table_ref[s0].astype(jnp.float32)
    p1 = table_ref[s1].astype(jnp.float32)
    q0 = pltpu.roll(p0, CELL, 1)
    q1 = pltpu.roll(p1, CELL, 1)
    parts = [
        jnp.where(left, p0, 0.0),
        jnp.where(left, q0, 0.0),
        jnp.where(left, 0.0, q1),
        jnp.where(left, 0.0, p1),
    ]
    split = jnp.concatenate(parts, axis=0).astype(jnp.bfloat16)
    placed = dot(rows_ref[fr], split).astype(jnp.bfloat16)
    return dot(placed, cols_ref[fc])


def image_kernel(emit_mask, inst_ref, orient_ref, owner_ref, table_ref, free_ref, rows_ref, cols_ref, *outs):
    a = pl.program_id(0)
    for pair in range(free_ref.shape[1] // LANES):
        codes = pair_codes(inst_ref, orient_ref, owner_ref, a, 2 * pair)
        cells = assemble_pair(table_ref, rows_ref, cols_ref, codes)
        lanes = slice(pair * LANES, (pair + 1) * LANES)
        value = jnp.tanh(cells + free_ref[:, lanes])
        outs[0][:, lanes] = value
        if emit_mask:
            outs[1][:, lanes] = value.astype(jnp.bfloat16)
            left = left_mask(HALF)
            if pair == 0:
                turned = pltpu.roll(value[HALF:], CELL, 1)
                outs[2][...] = jnp.where(left, value[:HALF], turned).astype(jnp.bfloat16)
            if pair == free_ref.shape[1] // LANES - 1:
                turned = pltpu.roll(value[:HALF], CELL, 1)
                outs[3][...] = jnp.where(left, turned, value[HALF:]).astype(jnp.bfloat16)


def whole_spec(array):
    zeros = (0,) * array.ndim
    return pl.BlockSpec(array.shape, lambda *_: zeros)


def image(inst, orient, owner, table, free, rows_place, cols_place, emit_mask):
    height, width = free.shape
    strip = pl.BlockSpec((CELL, width), lambda a, *_: (a, 0))
    out_shape = [jax.ShapeDtypeStruct(free.shape, jnp.float32)]
    out_specs = [strip]
    if emit_mask:
        edge = jax.ShapeDtypeStruct((height // 2, LANES), jnp.bfloat16)
        edge_spec = pl.BlockSpec((HALF, LANES), lambda a, *_: (a, 0))
        out_shape += [jax.ShapeDtypeStruct(free.shape, jnp.bfloat16), edge, edge]
        out_specs += [strip, edge_spec, edge_spec]
    return pl.pallas_call(
        functools.partial(image_kernel, emit_mask),
        grid_spec=pltpu.PrefetchScalarGridSpec(
            num_scalar_prefetch=3,
            grid=(height // CELL,),
            in_specs=[whole_spec(table), strip, whole_spec(rows_place), whole_spec(cols_place)],
            out_specs=out_specs,
        ),
        out_shape=out_shape,
        name="image",
    )(inst, orient, owner, table, free, rows_place, cols_place)


def tile_kernel(
    inst_ref, orient_ref, owner_ref, weights_ref,
    padded_ref, target_ref, shading_ref, free_ref, spectra_ref,
    cs_full_ref, cs_full_t_ref, cs_in_ref, cs_in_t_ref, field_ref, field_t_ref,
    rows_t_ref, cols_ref,
    resist_ref, new_free_ref, sums_ref,
    amp_s, half_s, bhalf_s, field_s, grad_s, sums_s,
):
    i = pl.program_id(0)
    j = pl.program_id(1)
    band = spectra_ref.shape[1]
    kernels = spectra_ref.shape[2]
    tile = target_ref.shape[0]
    pad_side = cs_full_ref.shape[1]
    pad_lanes = cs_full_t_ref.shape[0]
    block = field_s.shape[1]
    wide = 2 * band

    @pl.when((i == 0) & (j == 0))
    def _():
        sums_s[...] = jnp.zeros_like(sums_s)

    window = padded_ref[
        pl.ds(pl.multiple_of(i * tile, 128), pad_side), pl.ds(pl.multiple_of(j * tile, 128), pad_lanes)
    ]
    forw = dot(cs_full_ref[...], window).astype(jnp.bfloat16)
    spec = dot(forw, cs_full_t_ref[...])
    spec_re = (spec[:band, :band] + spec[band:, band:]) / pad_side
    spec_im = (spec[band:, :band] - spec[:band, band:]) / pad_side
    for k in range(kernels):
        kern_re = spectra_ref[0, :, k, :]
        kern_im = spectra_ref[1, :, k, :]
        amp_re = (kern_re * spec_re - kern_im * spec_im).astype(jnp.bfloat16)
        amp_im = (kern_re * spec_im + kern_im * spec_re).astype(jnp.bfloat16)
        at = k * wide
        amp_s[:band, at : at + band] = amp_re
        amp_s[band:, at : at + band] = -amp_im
        amp_s[:band, at + band : at + wide] = amp_im
        amp_s[band:, at + band : at + wide] = amp_re
    for k in range(kernels):
        cols = slice(k * wide, (k + 1) * wide)
        half_s[:, cols] = dot(cs_in_t_ref[...], amp_s[:, cols]).astype(jnp.bfloat16)

    def rows_step(n, carry):
        rows = pl.ds(pl.multiple_of(n * block, block), block)
        intensity = jnp.zeros((block, tile), jnp.float32)
        for k in range(kernels):
            field = dot(half_s[rows, k * wide : (k + 1) * wide], field_ref[...])
            field_s[k] = field
            re = field[:, :tile]
            im = field[:, tile:]
            intensity += (weights_ref[k] / (band * band)) * (re * re + im * im)
        resist = jax.nn.sigmoid(resist_gain * (intensity - resist_level))
        resist_ref[rows, :] = resist
        slopes = 2.0 * (resist - target_ref[rows, :]) * resist_gain * resist * (1.0 - resist)
        for k in range(kernels):
            scale = slopes * (2.0 * weights_ref[k] / (band * band))
            re = (field_s[k, :, :tile] * scale).astype(jnp.bfloat16)
            im = (field_s[k, :, tile:] * scale).astype(jnp.bfloat16)
            back = jnp.concatenate([re, im], axis=1)
            bhalf_s[rows, k * wide : (k + 1) * wide] = dot(back, field_t_ref[...]).astype(jnp.bfloat16)
        return carry

    lax.fori_loop(0, tile // block, rows_step, 0)
    bspec_re = jnp.zeros((band, band), jnp.float32)
    bspec_im = jnp.zeros((band, band), jnp.float32)
    for k in range(kernels):
        bamp = dot(cs_in_ref[...], bhalf_s[:, k * wide : (k + 1) * wide])
        bamp_re = bamp[:band, :band] + bamp[band:, band:]
        bamp_im = bamp[:band, band:] - bamp[band:, :band]
        kern_re = spectra_ref[0, :, k, :]
        kern_im = spectra_ref[1, :, k, :]
        bspec_re += kern_re * bamp_re + kern_im * bamp_im
        bspec_im += kern_re * bamp_im - kern_im * bamp_re
    bspec = jnp.concatenate([bspec_re / pad_side, bspec_im / pad_side], axis=1).astype(jnp.bfloat16)
    bforw = dot(bspec, field_ref[...]).astype(jnp.bfloat16)
    bforw = jnp.concatenate([bforw[:, :tile], bforw[:, tile:]], axis=0)
    gradient = dot(cs_in_t_ref[...], bforw)
    shading = shading_ref[...]
    grad_param = gradient * (1.0 - shading * shading)
    new_free_ref[...] = free_ref[...] - step_free * grad_param
    grad_s[...] = grad_param.astype(jnp.bfloat16)
    cells = tile // CELL
    left = left_mask(HALF)

    def cells_step(a, carry):
        rows = pl.ds(pl.multiple_of(a * CELL, CELL), CELL)
        for pair in range(cells // 2):
            s0, s1, fr, fc = pair_codes(
                inst_ref, orient_ref, owner_ref, i * cells + a, j * cells + 2 * pair
            )
            piece = grad_s[rows, pair * LANES : (pair + 1) * LANES]
            turned = dot(piece, cols_ref[fc]).astype(jnp.bfloat16)
            split = dot(rows_t_ref[fr], turned)
            a0 = split[:HALF]
            a1 = pltpu.roll(split[HALF : 2 * HALF], CELL, 1)
            b0 = pltpu.roll(split[2 * HALF : 3 * HALF], CELL, 1)
            b1 = split[3 * HALF :]
            sums_s[s0] += jnp.where(left, a0, a1)
            sums_s[s1] += jnp.where(left, b0, b1)
        return carry

    lax.fori_loop(0, cells, cells_step, 0)

    @pl.when((i == pl.num_programs(0) - 1) & (j == pl.num_programs(1) - 1))
    def _():
        sums_ref[...] = sums_s[...].astype(jnp.bfloat16)


def tile_steps(inst, orient, owner, weights, padded, target, shading, free, spectra, consts, rows_t, cols_place, masters):
    height, width = target.shape
    band = spectra.shape[1]
    kernels = spectra.shape[2]
    block = BLOCK
    tile_spec = pl.BlockSpec((TILE, TILE), lambda i, j, *_: (i, j))
    sums_shape = (masters, HALF, LANES)
    once = [padded, None, None, None, spectra, *consts, rows_t, cols_place]
    return pl.pallas_call(
        tile_kernel,
        grid_spec=pltpu.PrefetchScalarGridSpec(
            num_scalar_prefetch=4,
            grid=(height // TILE, width // TILE),
            in_specs=[tile_spec if v is None else whole_spec(v) for v in once],
            out_specs=[tile_spec, tile_spec, pl.BlockSpec(sums_shape, lambda *_: (0, 0, 0))],
            scratch_shapes=[
                pltpu.VMEM((2 * band, kernels * 2 * band), jnp.bfloat16),
                pltpu.VMEM((TILE, kernels * 2 * band), jnp.bfloat16),
                pltpu.VMEM((TILE, kernels * 2 * band), jnp.bfloat16),
                pltpu.VMEM((kernels, block, 2 * TILE), jnp.float32),
                pltpu.VMEM((TILE, TILE), jnp.bfloat16),
                pltpu.VMEM(sums_shape, jnp.float32),
            ],
        ),
        out_shape=[
            jax.ShapeDtypeStruct(target.shape, jnp.float32),
            jax.ShapeDtypeStruct(target.shape, jnp.float32),
            jax.ShapeDtypeStruct(sums_shape, jnp.bfloat16),
        ],
        compiler_params=pltpu.CompilerParams(vmem_limit_bytes=60 * 1024 * 1024),
        name="tile_steps",
    )(inst, orient, owner, weights, padded, target, shading, free, spectra, *consts, rows_t, cols_place)


MESH = pl.DeviceIdType.MESH
VM = pl.BlockSpec(memory_space=pltpu.VMEM)


def split_id(flat, n_col):
    return (lax.div(flat, n_col), lax.rem(flat, n_col))


def greet(peers):
    barrier = pltpu.get_barrier_semaphore()
    for peer in peers:
        pl.semaphore_signal(barrier, inc=1, device_id=peer, device_id_type=MESH)
    pl.semaphore_wait(barrier, len(peers))


def level_peers(n_row, n_col):
    r = lax.axis_index("row")
    c = lax.axis_index("col")
    long = n_col // 2
    z, y = lax.div(c, 2), lax.rem(c, 2)
    x, core = lax.div(r, 2), lax.rem(r, 2)
    p = x * 2 + y

    def z_at(t):
        return lax.rem(z + t + long, long)

    def p_at(t):
        q = lax.rem(p + t + n_row, n_row)
        return lax.div(q, 2), lax.rem(q, 2)

    return r, c, z, y, x, core, long, z_at, p_at


def gather_ids(n_row, n_col):
    r, c, z, y, x, core, long, z_at, p_at = level_peers(n_row, n_col)
    ids = [(r, z_at(t) * 2 + y) for t in range(1, long)]
    for t in range(1, n_row):
        px, py = p_at(t)
        ids.append((px * 2 + core, z * 2 + py))
    return ids + [(x * 2 + 1 - core, c)]


def gather_levels(n_row, n_col, own, table_ref, stored, send_sem, recv_sem):
    r, c, z, y, x, core, long, z_at, p_at = level_peers(n_row, n_col)
    share = stored // n_row

    def block(row, col):
        return table_ref.at[pl.ds(col * stored + row * share, share)]

    def make(src, dst, level, at, peer):
        return pltpu.make_async_remote_copy(
            src_ref=src,
            dst_ref=dst,
            send_sem=send_sem.at[level, at],
            recv_sem=recv_sem.at[level, at],
            device_id=peer,
            device_id_type=MESH,
        )

    partner = (x * 2 + 1 - core, c)
    mine = block(r, c)
    first = [make(own, mine, 0, t, (r, z_at(t) * 2 + y)) for t in range(1, long)]
    for copy in first:
        copy.start()
    second = []
    third = []
    for t in range(long):
        if t > 0:
            first[t - 1].wait_recv()
        here = block(r, z_at(-t) * 2 + y)
        src = own if t == 0 else here
        for q in range(1, n_row):
            px, py = p_at(q)
            copy = make(src, here, 1, t * n_row + q, (px * 2 + core, z * 2 + py))
            copy.start()
            second.append(copy)
        copy = make(src, here, 2, t * n_row, partner)
        copy.start()
        third.append(copy)
    for t in range(long):
        for q in range(1, n_row):
            second[t * (n_row - 1) + q - 1].wait_recv()
            px, py = p_at(-q)
            here = block(px * 2 + core, z_at(-t) * 2 + py)
            copy = make(here, here, 2, t * n_row + q, partner)
            copy.start()
            third.append(copy)
    for copy in third:
        copy.wait_recv()
    for copy in first + second + third:
        copy.wait_send()


def gather_sems(n_row, n_col):
    shape = (3, n_row * n_col // 2)
    return [pltpu.SemaphoreType.DMA(shape), pltpu.SemaphoreType.DMA(shape)]


def gather_kernel(n_row, n_col, own_ref, table_ref, send_sem, recv_sem):
    r = lax.axis_index("row")
    c = lax.axis_index("col")
    stored = own_ref.shape[0]
    share = stored // n_row
    greet(gather_ids(n_row, n_col))
    own = own_ref.at[pl.ds(r * share, share)]
    table_ref[pl.ds(c * stored + r * share, share)] = own_ref[pl.ds(r * share, share)]
    gather_levels(n_row, n_col, own, table_ref, stored, send_sem, recv_sem)


def gather_masters(own, n_row, n_col):
    return pl.pallas_call(
        functools.partial(gather_kernel, n_row, n_col),
        in_specs=[VM],
        out_specs=VM,
        out_shape=jax.ShapeDtypeStruct((n_col * own.shape[0],) + own.shape[1:], own.dtype),
        scratch_shapes=gather_sems(n_row, n_col),
        compiler_params=pltpu.CompilerParams(collective_id=0, has_side_effects=True),
        name="gather_masters",
    )(own)


def halo_kernel(
    n_row, n_col, mask_ref, edge_l_ref, edge_r_ref, out_ref, from_l, from_r, send_sem, recv_sem
):
    r = lax.axis_index("row")
    c = lax.axis_index("col")
    height, width = mask_ref.shape
    packed = height // 2
    middle = slice(LANES, LANES + width)
    row_parts = {
        -1: (slice(0, HALO), slice(HALO + height, 2 * HALO + height)),
        1: (slice(height - HALO, height), slice(0, HALO)),
    }
    edge_parts = {
        -1: (slice(0, HALF), slice(HALF + packed, 2 * HALF + packed)),
        0: (slice(0, packed), slice(HALF, HALF + packed)),
        1: (slice(packed - HALF, packed), slice(0, HALF)),
    }
    moves = [(0, 1), (0, -1), (1, 0), (-1, 0), (1, 1), (1, -1), (-1, 1), (-1, -1)]
    ids = [(lax.rem(r + n_row + dr, n_row), lax.rem(c + n_col + dc, n_col)) for dr, dc in moves]

    def inside(dr, dc):
        return (r + dr >= 0) & (r + dr < n_row) & (c + dc >= 0) & (c + dc < n_col)

    work = []
    for at, (dr, dc) in enumerate(moves):
        if dc == 0:
            src, dst = row_parts[dr]
            src, dst = mask_ref.at[src], out_ref.at[dst, middle]
        else:
            src, dst = edge_parts[dr]
            src = (edge_r_ref if dc == 1 else edge_l_ref).at[src]
            dst = (from_l if dc == 1 else from_r).at[dst]
        copy = pltpu.make_async_remote_copy(
            src_ref=src,
            dst_ref=dst,
            send_sem=send_sem.at[at],
            recv_sem=recv_sem.at[at],
            device_id=ids[at],
            device_id_type=MESH,
        )
        work.append((copy, dst, inside(dr, dc), inside(-dr, -dc)))
    greet(ids)
    for copy, dst, sends, gets in work:
        pl.when(sends)(copy.start)
    for copy, dst, sends, gets in work:

        @pl.when(jnp.logical_not(gets))
        def _():
            dst[...] = jnp.zeros(dst.shape, dst.dtype)

    out_ref[HALO : HALO + height, middle] = mask_ref[...]
    for copy, dst, sends, gets in work:
        pl.when(gets)(copy.wait_recv)
    left = left_mask(HALF)

    def unpack(a, carry):
        rows = pl.ds(pl.multiple_of(a * HALF, HALF), HALF)
        upper = pl.ds(pl.multiple_of(a * CELL, CELL), HALF)
        lower = pl.ds(pl.multiple_of(a * CELL + HALF, HALF), HALF)
        one = from_l[rows].astype(jnp.float32)
        two = from_r[rows].astype(jnp.float32)
        cast = lambda v: v.astype(jnp.bfloat16)
        last = slice(LANES + width, 2 * LANES + width)
        out_ref[upper, :LANES] = cast(jnp.where(left, 0.0, pltpu.roll(one, CELL, 1)))
        out_ref[lower, :LANES] = cast(jnp.where(left, 0.0, one))
        out_ref[upper, last] = cast(jnp.where(left, two, 0.0))
        out_ref[lower, last] = cast(jnp.where(left, pltpu.roll(two, CELL, 1), 0.0))
        return carry

    lax.fori_loop(0, (height + 2 * HALO) // CELL, unpack, 0)
    for copy, dst, sends, gets in work:
        pl.when(sends)(copy.wait_send)


def with_halo(mask, edge_l, edge_r, n_row, n_col):
    height, width = mask.shape
    return pl.pallas_call(
        functools.partial(halo_kernel, n_row, n_col),
        in_specs=[VM, VM, VM],
        out_specs=VM,
        out_shape=jax.ShapeDtypeStruct((height + 2 * HALO, width + 2 * LANES), mask.dtype),
        scratch_shapes=[
            pltpu.VMEM((height // 2 + 2 * HALF, LANES), mask.dtype),
            pltpu.VMEM((height // 2 + 2 * HALF, LANES), mask.dtype),
            pltpu.SemaphoreType.DMA((8,)),
            pltpu.SemaphoreType.DMA((8,)),
        ],
        compiler_params=pltpu.CompilerParams(collective_id=1, has_side_effects=True),
        name="with_halo",
    )(mask, edge_l, edge_r)


def smooth_packed(cells):
    count = cells.shape[0]
    flat = cells.reshape(count * HALF, LANES)
    lane = lax.broadcasted_iota(jnp.int32, flat.shape, 1)
    x = lane % CELL
    row = lax.broadcasted_iota(jnp.int32, flat.shape, 0) % HALF
    before = jnp.where(x == 0, 0.0, pltpu.roll(flat, 1, 1))
    after = jnp.where(x == CELL - 1, 0.0, pltpu.roll(flat, LANES - 1, 1))
    other = pltpu.roll(flat, CELL, 1)
    up = jnp.where(row == 0, 0.0, pltpu.roll(other, 1, 0))
    down = jnp.where(row == HALF - 1, 0.0, pltpu.roll(other, count * HALF - 1, 0))
    beside = before + after + other + jnp.where(lane < CELL, up, down)
    return (0.5 * flat + 0.125 * beside).reshape(cells.shape)


def update_kernel(
    n_row, n_col, sums_ref, own_ref, table_ref,
    parts, fresh, send_sem, recv_sem, send2_sem, recv2_sem,
):
    r = lax.axis_index("row")
    c = lax.axis_index("col")
    count = n_row * n_col
    me = r * n_col + c
    stored = own_ref.shape[0]
    share = stored // n_row
    barrier = pltpu.get_barrier_semaphore()

    def first_row(flat):
        pr, pc = split_id(flat, n_col)
        return pc * stored + pr * share

    def hello(t, carry):
        pl.semaphore_signal(
            barrier, inc=1, device_id=split_id(lax.rem(me + t, count), n_col), device_id_type=MESH
        )
        return carry

    lax.fori_loop(1, count, hello, 0)
    pl.semaphore_wait(barrier, count - 1)

    def part_copy(t):
        peer = lax.rem(me + t, count)
        return pltpu.make_async_remote_copy(
            src_ref=sums_ref.at[pl.ds(first_row(peer), share)],
            dst_ref=parts.at[t],
            send_sem=send_sem.at[t],
            recv_sem=recv_sem.at[t],
            device_id=split_id(peer, n_col),
            device_id_type=MESH,
        )

    def start_part(t, carry):
        part_copy(t).start()
        return carry

    lax.fori_loop(1, count, start_part, 0)

    def add_part(t, total):
        part_copy(t).wait_recv()
        return total + parts[t].astype(jnp.float32)

    mine = first_row(me)
    total = lax.fori_loop(1, count, add_part, sums_ref[pl.ds(mine, share)].astype(jnp.float32))
    updated = own_ref[pl.ds(r * share, share)] - step_master * total
    value = smooth_packed(updated).astype(jnp.bfloat16)
    fresh[...] = value
    table_ref[pl.ds(mine, share)] = value

    def end_part(t, carry):
        part_copy(t).wait_send()
        return carry

    lax.fori_loop(1, count, end_part, 0)

    gather_levels(n_row, n_col, fresh, table_ref, stored, send2_sem, recv2_sem)


def update_masters(sums, own, n_row, n_col):
    count = n_row * n_col
    piece = (own.shape[0] // n_row,) + own.shape[1:]
    return pl.pallas_call(
        functools.partial(update_kernel, n_row, n_col),
        in_specs=[VM, VM],
        out_specs=VM,
        out_shape=jax.ShapeDtypeStruct(sums.shape, jnp.bfloat16),
        scratch_shapes=[
            pltpu.VMEM((count,) + piece, jnp.bfloat16),
            pltpu.VMEM(piece, jnp.bfloat16),
            pltpu.SemaphoreType.DMA((count,)),
            pltpu.SemaphoreType.DMA((count,)),
            *gather_sems(n_row, n_col),
        ],
        compiler_params=pltpu.CompilerParams(collective_id=2, has_side_effects=True),
        name="update_masters",
    )(sums, own)


def per_device(
    masters, inst_master, inst_orient, owner_map, tile_free, target, kernel_spectra, socs_weights
):
    stored = masters.shape[0]
    total = owner_map.shape[0]
    consts = tables(TILE + 2 * HALO, kernel_spectra.shape[1], HALO, TILE)
    rows_place, rows_t, cols_place = placements()
    own = masters.reshape(stored, HALF, LANES)
    n_row = lax.axis_size("row")
    n_col = lax.axis_size("col")
    table = gather_masters(own.astype(jnp.bfloat16), n_row, n_col)
    shading, mask, edge_l, edge_r = image(
        inst_master, inst_orient, owner_map, table, tile_free, rows_place, cols_place, True
    )
    padded = with_halo(mask, edge_l, edge_r, n_row, n_col)
    resist, new_free, sums = tile_steps(
        inst_master, inst_orient, owner_map, socs_weights, padded, target, shading, tile_free,
        kernel_spectra, consts, rows_t, cols_place, total,
    )
    table = update_masters(sums, own, n_row, n_col)
    fresh = lax.dynamic_slice_in_dim(table, lax.axis_index("col") * stored, stored, 0)
    (new_mask,) = image(
        inst_master, inst_orient, owner_map, table, new_free, rows_place, cols_place, False
    )
    return (resist, new_mask, fresh.astype(jnp.float32).reshape(masters.shape))


def solution(mesh):
    in_specs = (
        P("col", None),
        P("row", "col"),
        P("row", "col"),
        P(),
        P("row", "col"),
        P("row", "col"),
        P(),
        P(),
    )
    out_specs = (P("row", "col"), P("row", "col"), P("col", None))
    return jax.shard_map(
        per_device, mesh=mesh, in_specs=in_specs, out_specs=out_specs, check_vma=False
    )
```

profile of v0, /device:TPU:0, one launch (start us, length us, event | category | flops | bytes accessed | tf_op | source)
XLA Modules:
  0.0 180.8 jit_solution(6561766693534998162)
XLA Ops:
  0.6 1.0 copy.20
  1.6 0.0 copy-start
  1.6 0.7 bitcast_convert_fusion.own_ref
  2.4 17.5 %gather_masters.1.table_ref = bf16[128,32,128]{2,1,0:T(8,128)(2,1)} custom-call(bf16[16,32,128]{2,1,0:T(8,128)(2,1)} %bitcast_convert_fusion.own_ref), custom_call_target="tpu_custom_call" | custom-call | tf_op jit(solution)/shard_map/gather_masters/pallas_call | solution.py:392
  19.9 15.2 %image.2 = (f32[1024,1024]{1,0:T(8,128)}, bf16[1024,1024]{1,0:T(8,128)(2,1)}, bf16[512,128]{1,0:T(8,128)(2,1)}, bf16[512,128]{1,0:T(8,128)(2,1)}) custom-call(s32[16,16]{1,0:T(8,128)} %inst_ref.5, s32[16,16]{1,0:T(8,128)} %orient_ref.5, s32[128]{0:T(128)} %owner_ref.5, bf16[128,32,128]{2,1,0:T(8,128)(2,1)} %gather_masters.1.table_ref, ...), custom_call_target="tpu_custom_call" | custom-call | tf_op jit(solution)/shard_map/image/pallas_call | solution.py:126
  35.1 13.2 %with_halo.1.padded_ref = bf16[1152,1280]{1,0:T(8,128)(2,1)} custom-call(bf16[1024,1024]{1,0:T(8,128)(2,1)} %get-tuple-element.10.mask_ref, bf16[512,128]{1,0:T(8,128)(2,1)} %get-tuple-element.11.edge_l_ref, bf16[512,128]{1,0:T(8,128)(2,1)} %get-tuple-element.12.edge_r_ref), custom_call_target="tpu_custom_call" | custom-call | tf_op jit(solution)/shard_map/with_halo/pallas_call | solution.py:479
  48.3 0.0 copy-done
  48.3 71.1 %tile_steps.1 = (f32[1024,1024]{1,0:T(8,128)}, f32[1024,1024]{1,0:T(8,128)}, bf16[128,32,128]{2,1,0:T(8,128)(2,1)}) custom-call(s32[16,16]{1,0:T(8,128)} %inst_ref.5, s32[16,16]{1,0:T(8,128)} %orient_ref.5, s32[128]{0:T(128)} %owner_ref.5, f32[8]{0:T(128)} %weights_ref.1, bf16[1152,1280]{1,0:T(8,128)(2,1)} %with_halo.1.padded_ref, f32[1024,1024]{1,0:T(8,128)} %target_ref.1, ...), custom_call_target="tpu_custom_call" | custom-call | tf_op jit(solution)/shard_map/tile_steps/pallas_call | solution.py:256
  119.4 44.7 %update_masters.1.table_ref = bf16[128,32,128]{2,1,0:T(8,128)(2,1)} custom-call(bf16[128,32,128]{2,1,0:T(8,128)(2,1)} %get-tuple-element.15.sums_ref, f32[16,32,128]{2,1,0:T(8,128)} %bitcast.7), custom_call_target="tpu_custom_call" | custom-call | tf_op jit(solution)/shard_map/update_masters/pallas_call | solution.py:575
  164.2 14.8 %image.3 = f32[1024,1024]{1,0:T(8,128)} custom-call(s32[16,16]{1,0:T(8,128)} %inst_ref.5, s32[16,16]{1,0:T(8,128)} %orient_ref.5, s32[128]{0:T(128)} %owner_ref.5, bf16[128,32,128]{2,1,0:T(8,128)(2,1)} %update_masters.1.table_ref, f32[1024,1024]{1,0:T(8,128)} %get-tuple-element.16.free_ref, bf16[4,64,128]{2,1,0:T(8,128)(2,1)} %constant.34.clone.rows_ref, ...), custom_call_target="tpu_custom_call" | custom-call | tf_op jit(solution)/shard_map/image/pallas_call | solution.py:126
  179.0 0.9 dynamic-slice_convert_fusion
  179.9 0.9 copy.23
Async XLA Ops:
  1.6 46.7 %copy-start = (f32[2,8,32,128]{3,2,1,0:T(8,128)}, f32[2,8,32,128]{3,2,1,0:T(8,128)S(1)}, u32[]{:S(2)}) copy-start(f32[2,8,32,128]{3,2,1,0:T(8,128)S(1)} %copy.20) | copy-start | bytes 786436
where the time goes:
time: 182 us; the launch traced here: 181 us
  Pallas kernels  177 us (97%)
  local copies, waits for them, and re-layouts  1.87 us (1%)
    pallas_call x1, Pallas kernels, tile_steps(): pl.pallas_call(tile_kernel, grid_spec=pltpu.PrefetchScalarGridSpec(num_sc...  71.1 us
    pallas_call x1, Pallas kernels, update_masters(): pl.pallas_call(functools.partial(update_kernel, n_row, n_col), in_specs=[...  44.7 us
    pallas_call x2, Pallas kernels, image(): pl.pallas_call(functools.partial(image_kernel, emit_mask), grid_spec=pltp...  30 us
    pallas_call x1, Pallas kernels, gather_masters(): pl.pallas_call(functools.partial(gather_kernel, n_row, n_col), in_specs=[...  17.5 us
    pallas_call x1, Pallas kernels, with_halo(): pl.pallas_call(functools.partial(halo_kernel, n_row, n_col), in_specs=[VM...  13.2 us

commit v1 on v0

--- a/solution.py
+++ b/solution.py
@@ -15,7 +15,8 @@
 CELL = 64
 LANES = 128
 HALF = CELL // 2
-BLOCK = 512
+STRIP = 16
+GROUP = 4
 
 step_free = 1.0
 step_master = 0.05
@@ -25,6 +26,10 @@
 
 def dot(left, right):
     return jnp.dot(left, right, preferred_element_type=jnp.float32)
+
+
+def bfloat(value):
+    return jnp.asarray(np.ascontiguousarray(value).astype(jnp.bfloat16))
 
 
 def tables(pad_side, band_side, halo, tile):
@@ -38,25 +43,30 @@
     cs_full = np.concatenate([cos, sin], 0)
     cs_lanes = np.pad(cs_full, ((0, 0), (LANES - halo, LANES - halo)))
     cs_in = np.concatenate([cos_in, sin_in], 0)
-    field = np.block([[cos_in, sin_in], [-sin_in, cos_in]])
-    parts = (cs_full, cs_lanes.T, cs_in, cs_in.T, field, field.T)
-    return [jnp.asarray(np.ascontiguousarray(p).astype(jnp.bfloat16)) for p in parts]
-
-
-def placements():
-    rows_place = np.zeros((4, CELL, 2 * CELL), np.float32)
-    cols_place = np.zeros((4, LANES, LANES), np.float32)
-    for f in range(4):
-        for side in range(2):
-            flip = (f >> side) & 1
-            for r in range(HALF):
-                for h in range(2):
-                    y = 2 * r + h
-                    rows_place[f, CELL - 1 - y if flip else y, side * CELL + h * HALF + r] = 1
-            for x in range(CELL):
-                cols_place[f, side * CELL + x, side * CELL + (CELL - 1 - x if flip else x)] = 1
-    cast = lambda v: jnp.asarray(np.ascontiguousarray(v).astype(jnp.bfloat16))
-    return cast(rows_place), cast(rows_place.transpose(0, 2, 1)), cast(cols_place)
+    grid = 2 * band_side
+    turns = (freqs[:, None] * np.arange(grid)[None, :]) % grid
+    cos_g = np.cos(turns * (2.0 * math.pi / grid))
+    sin_g = np.sin(turns * (2.0 * math.pi / grid))
+    cs_g = np.concatenate([cos_g, sin_g], 0)
+    field = np.block([[cos_g, sin_g], [-sin_g, cos_g]])
+    gaps = np.arange(halo, halo + tile)[:, None] / pad_side - np.arange(grid)[None, :] / grid
+    waves = np.arange(1, band_side)
+    spread = (1.0 + 2.0 * np.cos(2.0 * math.pi * gaps[:, :, None] * waves).sum(-1)) / grid
+    parts = (cs_full, cs_lanes.T, cs_g, cs_g.T, field, field.T, spread, spread.T, cs_in, cs_in.T)
+    return [bfloat(p) for p in parts]
+
+
+def flips():
+    back = np.eye(CELL)[::-1]
+    rows = np.kron(np.eye(4), back)
+    same = np.eye(CELL)
+    none = np.zeros((CELL, CELL))
+    spread = [
+        np.block([[m, m], [none, none]]) if e == 0 else np.block([[none, none], [m, m]])
+        for m in (same, back)
+        for e in range(2)
+    ]
+    return bfloat(rows), bfloat(np.concatenate(spread, 1))
 
 
 def left_mask(rows):
@@ -66,46 +76,57 @@
 def pair_codes(inst_ref, orient_ref, owner_ref, a, b):
     s0 = owner_ref[inst_ref[a, b]]
     s1 = owner_ref[inst_ref[a, b + 1]]
-    o0 = orient_ref[a, b]
-    o1 = orient_ref[a, b + 1]
-    return s0, s1, (o0 & 1) + 2 * (o1 & 1), (o0 >> 1) + 2 * (o1 >> 1)
-
-
-def assemble_pair(table_ref, rows_ref, cols_ref, codes):
-    s0, s1, fr, fc = codes
-    left = left_mask(HALF)
-    p0 = table_ref[s0].astype(jnp.float32)
-    p1 = table_ref[s1].astype(jnp.float32)
-    q0 = pltpu.roll(p0, CELL, 1)
-    q1 = pltpu.roll(p1, CELL, 1)
-    parts = [
-        jnp.where(left, p0, 0.0),
-        jnp.where(left, q0, 0.0),
-        jnp.where(left, 0.0, q1),
-        jnp.where(left, 0.0, p1),
-    ]
-    split = jnp.concatenate(parts, axis=0).astype(jnp.bfloat16)
-    placed = dot(rows_ref[fr], split).astype(jnp.bfloat16)
-    return dot(placed, cols_ref[fc])
-
-
-def image_kernel(emit_mask, inst_ref, orient_ref, owner_ref, table_ref, free_ref, rows_ref, cols_ref, *outs):
+    return s0, s1, orient_ref[a, b], orient_ref[a, b + 1]
+
+
+def build_turned(table_ref, turned_ref, flip_ref, spread_ref):
+    def step(b, carry):
+        at = pl.ds(b * 4, 4)
+        cells = table_ref[at].reshape(4 * CELL, LANES)
+        flipped = dot(flip_ref[...], cells).astype(jnp.bfloat16)
+        for f, part in enumerate((cells, flipped)):
+            both = dot(part, spread_ref[...]).astype(jnp.bfloat16)
+            for c in range(2):
+                for e in range(2):
+                    lanes = slice((2 * c + e) * LANES, (2 * c + e + 1) * LANES)
+                    turned_ref[2 * c + f, at, e] = both[:, lanes].reshape(4, CELL, LANES)
+        return carry
+
+    lax.fori_loop(0, table_ref.shape[0] // 4, step, 0)
+
+
+def assemble_pair(turned_ref, codes):
+    s0, s1, o0, o1 = codes
+    one = turned_ref[o0, s0 // 2, s0 % 2].astype(jnp.float32)
+    two = turned_ref[o1, s1 // 2, s1 % 2].astype(jnp.float32)
+    return jnp.where(left_mask(CELL), one, two)
+
+
+def image_kernel(
+    emit_mask, inst_ref, orient_ref, owner_ref, table_ref, free_ref, flip_ref, spread_ref, *rest
+):
+    *outs, turned_s = rest
     a = pl.program_id(0)
-    for pair in range(free_ref.shape[1] // LANES):
+
+    @pl.when(a == 0)
+    def _():
+        build_turned(table_ref, turned_s, flip_ref, spread_ref)
+
+    pairs = free_ref.shape[1] // LANES
+    for pair in range(pairs):
         codes = pair_codes(inst_ref, orient_ref, owner_ref, a, 2 * pair)
-        cells = assemble_pair(table_ref, rows_ref, cols_ref, codes)
+        cells = assemble_pair(turned_s, codes)
         lanes = slice(pair * LANES, (pair + 1) * LANES)
         value = jnp.tanh(cells + free_ref[:, lanes])
-        outs[0][:, lanes] = value
+        outs[0][:, lanes] = value.astype(outs[0].dtype)
         if emit_mask:
-            outs[1][:, lanes] = value.astype(jnp.bfloat16)
             left = left_mask(HALF)
             if pair == 0:
                 turned = pltpu.roll(value[HALF:], CELL, 1)
-                outs[2][...] = jnp.where(left, value[:HALF], turned).astype(jnp.bfloat16)
-            if pair == free_ref.shape[1] // LANES - 1:
+                outs[1][...] = jnp.where(left, value[:HALF], turned).astype(jnp.bfloat16)
+            if pair == pairs - 1:
                 turned = pltpu.roll(value[:HALF], CELL, 1)
-                outs[3][...] = jnp.where(left, turned, value[HALF:]).astype(jnp.bfloat16)
+                outs[2][...] = jnp.where(left, turned, value[HALF:]).astype(jnp.bfloat16)
 
 
 def whole_spec(array):
@@ -113,36 +134,37 @@
     return pl.BlockSpec(array.shape, lambda *_: zeros)
 
 
-def image(inst, orient, owner, table, free, rows_place, cols_place, emit_mask):
+def image(inst, orient, owner, table, free, flip, spread, emit_mask):
     height, width = free.shape
     strip = pl.BlockSpec((CELL, width), lambda a, *_: (a, 0))
-    out_shape = [jax.ShapeDtypeStruct(free.shape, jnp.float32)]
+    out_shape = [jax.ShapeDtypeStruct(free.shape, jnp.bfloat16 if emit_mask else jnp.float32)]
     out_specs = [strip]
     if emit_mask:
         edge = jax.ShapeDtypeStruct((height // 2, LANES), jnp.bfloat16)
         edge_spec = pl.BlockSpec((HALF, LANES), lambda a, *_: (a, 0))
-        out_shape += [jax.ShapeDtypeStruct(free.shape, jnp.bfloat16), edge, edge]
-        out_specs += [strip, edge_spec, edge_spec]
+        out_shape += [edge, edge]
+        out_specs += [edge_spec, edge_spec]
     return pl.pallas_call(
         functools.partial(image_kernel, emit_mask),
         grid_spec=pltpu.PrefetchScalarGridSpec(
             num_scalar_prefetch=3,
             grid=(height // CELL,),
-            in_specs=[whole_spec(table), strip, whole_spec(rows_place), whole_spec(cols_place)],
+            in_specs=[whole_spec(table), strip, whole_spec(flip), whole_spec(spread)],
             out_specs=out_specs,
+            scratch_shapes=[pltpu.VMEM((4, table.shape[0], 2, CELL, LANES), jnp.bfloat16)],
         ),
         out_shape=out_shape,
         name="image",
-    )(inst, orient, owner, table, free, rows_place, cols_place)
+    )(inst, orient, owner, table, free, flip, spread)
 
 
 def tile_kernel(
     inst_ref, orient_ref, owner_ref, weights_ref,
-    padded_ref, target_ref, shading_ref, free_ref, spectra_ref,
-    cs_full_ref, cs_full_t_ref, cs_in_ref, cs_in_t_ref, field_ref, field_t_ref,
-    rows_t_ref, cols_ref,
+    padded_ref, target_ref, free_ref, spectra_ref,
+    cs_full_ref, cs_lanes_t_ref, cs_g_ref, cs_g_t_ref, field_ref, field_t_ref,
+    spread_ref, spread_t_ref, cs_in_ref, cs_in_t_ref, flip_ref,
     resist_ref, new_free_ref, sums_ref,
-    amp_s, half_s, bhalf_s, field_s, grad_s, sums_s,
+    kern_s, half_s, field_s, bhalf_s, level_s, turned_s, sums_s,
 ):
     i = pl.program_id(0)
     j = pl.program_id(1)
@@ -150,109 +172,126 @@
     kernels = spectra_ref.shape[2]
     tile = target_ref.shape[0]
     pad_side = cs_full_ref.shape[1]
-    pad_lanes = cs_full_t_ref.shape[0]
-    block = field_s.shape[1]
-    wide = 2 * band
+    pad_lanes = cs_lanes_t_ref.shape[0]
+    grid = 2 * band
+    blocks = grid // STRIP
+    low = lambda v: v.astype(jnp.bfloat16)
 
     @pl.when((i == 0) & (j == 0))
     def _():
         sums_s[...] = jnp.zeros_like(sums_s)
-
+        for k in range(kernels):
+            weight = jnp.full((band, LANES), weights_ref[k], jnp.float32)
+            scale = jnp.sqrt(weight) / (pad_side * band)
+            for part in range(2):
+                kern_s[part, k] = spectra_ref[part, :, k, :] * scale
+
+    at_row = i * tile
+    at_col = j * tile
     window = padded_ref[
-        pl.ds(pl.multiple_of(i * tile, 128), pad_side), pl.ds(pl.multiple_of(j * tile, 128), pad_lanes)
+        pl.ds(pl.multiple_of(at_row, 128), pad_side), pl.ds(pl.multiple_of(at_col, 128), pad_lanes)
     ]
-    forw = dot(cs_full_ref[...], window).astype(jnp.bfloat16)
-    spec = dot(forw, cs_full_t_ref[...])
-    spec_re = (spec[:band, :band] + spec[band:, band:]) / pad_side
-    spec_im = (spec[band:, :band] - spec[:band, band:]) / pad_side
+    forw = low(dot(cs_full_ref[...], window))
+    spec = dot(forw, cs_lanes_t_ref[...])
+    spec_re = spec[:band, :band] + spec[band:, band:]
+    spec_im = spec[band:, :band] - spec[:band, band:]
     for k in range(kernels):
-        kern_re = spectra_ref[0, :, k, :]
-        kern_im = spectra_ref[1, :, k, :]
-        amp_re = (kern_re * spec_re - kern_im * spec_im).astype(jnp.bfloat16)
-        amp_im = (kern_re * spec_im + kern_im * spec_re).astype(jnp.bfloat16)
-        at = k * wide
-        amp_s[:band, at : at + band] = amp_re
-        amp_s[band:, at : at + band] = -amp_im
-        amp_s[:band, at + band : at + wide] = amp_im
-        amp_s[band:, at + band : at + wide] = amp_re
-    for k in range(kernels):
-        cols = slice(k * wide, (k + 1) * wide)
-        half_s[:, cols] = dot(cs_in_t_ref[...], amp_s[:, cols]).astype(jnp.bfloat16)
-
-    def rows_step(n, carry):
-        rows = pl.ds(pl.multiple_of(n * block, block), block)
-        intensity = jnp.zeros((block, tile), jnp.float32)
-        for k in range(kernels):
-            field = dot(half_s[rows, k * wide : (k + 1) * wide], field_ref[...])
-            field_s[k] = field
-            re = field[:, :tile]
-            im = field[:, tile:]
-            intensity += (weights_ref[k] / (band * band)) * (re * re + im * im)
-        resist = jax.nn.sigmoid(resist_gain * (intensity - resist_level))
-        resist_ref[rows, :] = resist
-        slopes = 2.0 * (resist - target_ref[rows, :]) * resist_gain * resist * (1.0 - resist)
-        for k in range(kernels):
-            scale = slopes * (2.0 * weights_ref[k] / (band * band))
-            re = (field_s[k, :, :tile] * scale).astype(jnp.bfloat16)
-            im = (field_s[k, :, tile:] * scale).astype(jnp.bfloat16)
-            back = jnp.concatenate([re, im], axis=1)
-            bhalf_s[rows, k * wide : (k + 1) * wide] = dot(back, field_t_ref[...]).astype(jnp.bfloat16)
-        return carry
-
-    lax.fori_loop(0, tile // block, rows_step, 0)
+        amp_re = low(kern_s[0, k] * spec_re - kern_s[1, k] * spec_im)
+        amp_im = low(kern_s[0, k] * spec_im + kern_s[1, k] * spec_re)
+        upper = jnp.concatenate([amp_re, amp_im], axis=1)
+        lower = jnp.concatenate([-amp_im, amp_re], axis=1)
+        half = low(dot(cs_g_t_ref[...], jnp.concatenate([upper, lower], axis=0)))
+        half_s[:, k] = half.reshape(blocks, STRIP, grid)
+    for b in range(0, blocks, GROUP):
+        lines = half_s[b : b + GROUP].reshape(GROUP * kernels * STRIP, grid)
+        field = dot(lines, field_ref[...])
+        re = field[:, :grid]
+        im = field[:, grid:]
+        power = (re * re + im * im).reshape(GROUP, kernels, STRIP, grid)
+        level_s[b : b + GROUP] = jnp.sum(power, axis=1)
+        field_s[b : b + GROUP] = low(field).reshape(GROUP, kernels, STRIP, 2 * grid)
+    level = level_s[...].reshape(grid, grid)
+    mean = jnp.sum(jnp.sum(level, axis=0, keepdims=True), axis=1, keepdims=True) / (grid * grid)
+    lines = low(dot(spread_ref[...], low(level - mean)))
+    intensity = dot(lines, spread_t_ref[...]) + mean
+    resist = jax.nn.sigmoid(resist_gain * (intensity - resist_level))
+    resist_ref[...] = resist
+    slopes = (4.0 * resist_gain) * (resist - target_ref[...]) * resist * (1.0 - resist)
+    lines = low(dot(spread_t_ref[...], low(slopes)))
+    level_s[...] = dot(lines, spread_ref[...]).reshape(blocks, STRIP, grid)
+    for b in range(0, blocks, GROUP):
+        pull = level_s[b : b + GROUP].reshape(GROUP, 1, STRIP, grid)
+        pull = jnp.concatenate([pull, pull], axis=3)
+        back = low(field_s[b : b + GROUP].astype(jnp.float32) * pull)
+        bhalf = low(dot(back.reshape(GROUP * kernels * STRIP, 2 * grid), field_t_ref[...]))
+        bhalf = bhalf.reshape(GROUP, kernels, STRIP, grid)
+        for g in range(GROUP):
+            bhalf_s[:, b + g] = bhalf[g]
     bspec_re = jnp.zeros((band, band), jnp.float32)
     bspec_im = jnp.zeros((band, band), jnp.float32)
     for k in range(kernels):
-        bamp = dot(cs_in_ref[...], bhalf_s[:, k * wide : (k + 1) * wide])
+        bamp = dot(cs_g_ref[...], bhalf_s[k].reshape(grid, grid))
         bamp_re = bamp[:band, :band] + bamp[band:, band:]
         bamp_im = bamp[:band, band:] - bamp[band:, :band]
-        kern_re = spectra_ref[0, :, k, :]
-        kern_im = spectra_ref[1, :, k, :]
-        bspec_re += kern_re * bamp_re + kern_im * bamp_im
-        bspec_im += kern_re * bamp_im - kern_im * bamp_re
-    bspec = jnp.concatenate([bspec_re / pad_side, bspec_im / pad_side], axis=1).astype(jnp.bfloat16)
-    bforw = dot(bspec, field_ref[...]).astype(jnp.bfloat16)
-    bforw = jnp.concatenate([bforw[:, :tile], bforw[:, tile:]], axis=0)
+        bspec_re += kern_s[0, k] * bamp_re + kern_s[1, k] * bamp_im
+        bspec_im += kern_s[0, k] * bamp_im - kern_s[1, k] * bamp_re
+    upper = jnp.concatenate([low(bspec_re), low(-bspec_im)], axis=1)
+    lower = jnp.concatenate([low(bspec_im), low(bspec_re)], axis=1)
+    bforw = low(dot(jnp.concatenate([upper, lower], axis=0), cs_in_ref[...]))
     gradient = dot(cs_in_t_ref[...], bforw)
-    shading = shading_ref[...]
+    shading = padded_ref[
+        pl.ds(pl.multiple_of(at_row + HALO, HALO), tile), pl.ds(pl.multiple_of(at_col + LANES, LANES), tile)
+    ].astype(jnp.float32)
     grad_param = gradient * (1.0 - shading * shading)
     new_free_ref[...] = free_ref[...] - step_free * grad_param
-    grad_s[...] = grad_param.astype(jnp.bfloat16)
+    turned_s[0] = grad_param
+    plain = low(grad_param)
+    group = flip_ref.shape[0]
+    for at in range(0, tile, group):
+        part = slice(at, at + group)
+        across = dot(plain[:, part], flip_ref[...])
+        turned_s[2, :, part] = across
+        for f, source in ((1, plain[:, part]), (3, low(across))):
+            for up in range(0, tile, group):
+                turned_s[f, up : up + group, part] = dot(flip_ref[...], source[up : up + group])
     cells = tile // CELL
-    left = left_mask(HALF)
+    left = left_mask(CELL)
 
     def cells_step(a, carry):
         rows = pl.ds(pl.multiple_of(a * CELL, CELL), CELL)
         for pair in range(cells // 2):
-            s0, s1, fr, fc = pair_codes(
+            s0, s1, o0, o1 = pair_codes(
                 inst_ref, orient_ref, owner_ref, i * cells + a, j * cells + 2 * pair
             )
-            piece = grad_s[rows, pair * LANES : (pair + 1) * LANES]
-            turned = dot(piece, cols_ref[fc]).astype(jnp.bfloat16)
-            split = dot(rows_t_ref[fr], turned)
-            a0 = split[:HALF]
-            a1 = pltpu.roll(split[HALF : 2 * HALF], CELL, 1)
-            b0 = pltpu.roll(split[2 * HALF : 3 * HALF], CELL, 1)
-            b1 = split[3 * HALF :]
-            sums_s[s0] += jnp.where(left, a0, a1)
-            sums_s[s1] += jnp.where(left, b0, b1)
+            lanes = slice(pair * LANES, (pair + 1) * LANES)
+            sums_s[s0] += jnp.where(left, turned_s[o0, rows, lanes], 0.0)
+            sums_s[s1] += jnp.where(left, 0.0, turned_s[o1, rows, lanes])
         return carry
 
     lax.fori_loop(0, cells, cells_step, 0)
 
     @pl.when((i == pl.num_programs(0) - 1) & (j == pl.num_programs(1) - 1))
     def _():
-        sums_ref[...] = sums_s[...].astype(jnp.bfloat16)
-
-
-def tile_steps(inst, orient, owner, weights, padded, target, shading, free, spectra, consts, rows_t, cols_place, masters):
+        def pack(p, carry):
+            one = sums_s[2 * p]
+            two = sums_s[2 * p + 1]
+            one = one + pltpu.roll(one, CELL, 1)
+            two = two + pltpu.roll(two, CELL, 1)
+            sums_ref[p] = low(jnp.where(left, one, two))
+            return carry
+
+        lax.fori_loop(0, sums_ref.shape[0], pack, 0)
+
+
+def tile_steps(inst, orient, owner, weights, padded, target, free, spectra, consts, flip, masters):
     height, width = target.shape
     band = spectra.shape[1]
     kernels = spectra.shape[2]
-    block = BLOCK
+    grid = 2 * band
+    blocks = grid // STRIP
     tile_spec = pl.BlockSpec((TILE, TILE), lambda i, j, *_: (i, j))
-    sums_shape = (masters, HALF, LANES)
-    once = [padded, None, None, None, spectra, *consts, rows_t, cols_place]
+    sums_shape = (masters // 2, CELL, LANES)
+    once = [padded, None, None, spectra, *consts, flip]
     return pl.pallas_call(
         tile_kernel,
         grid_spec=pltpu.PrefetchScalarGridSpec(
@@ -261,12 +300,13 @@
             in_specs=[tile_spec if v is None else whole_spec(v) for v in once],
             out_specs=[tile_spec, tile_spec, pl.BlockSpec(sums_shape, lambda *_: (0, 0, 0))],
             scratch_shapes=[
-                pltpu.VMEM((2 * band, kernels * 2 * band), jnp.bfloat16),
-                pltpu.VMEM((TILE, kernels * 2 * band), jnp.bfloat16),
-                pltpu.VMEM((TILE, kernels * 2 * band), jnp.bfloat16),
-                pltpu.VMEM((kernels, block, 2 * TILE), jnp.float32),
-                pltpu.VMEM((TILE, TILE), jnp.bfloat16),
-                pltpu.VMEM(sums_shape, jnp.float32),
+                pltpu.VMEM((2, kernels, band, band), jnp.float32),
+                pltpu.VMEM((blocks, kernels, STRIP, grid), jnp.bfloat16),
+                pltpu.VMEM((blocks, kernels, STRIP, 2 * grid), jnp.bfloat16),
+                pltpu.VMEM((kernels, blocks, STRIP, grid), jnp.bfloat16),
+                pltpu.VMEM((blocks, STRIP, grid), jnp.float32),
+                pltpu.VMEM((4, TILE, TILE), jnp.float32),
+                pltpu.VMEM((masters, CELL, LANES), jnp.float32),
             ],
         ),
         out_shape=[
@@ -276,7 +316,7 @@
         ],
         compiler_params=pltpu.CompilerParams(vmem_limit_bytes=60 * 1024 * 1024),
         name="tile_steps",
-    )(inst, orient, owner, weights, padded, target, shading, free, spectra, *consts, rows_t, cols_place)
+    )(inst, orient, owner, weights, padded, target, free, spectra, *consts, flip)
 
 
 MESH = pl.DeviceIdType.MESH
@@ -494,17 +534,14 @@
 
 def smooth_packed(cells):
     count = cells.shape[0]
-    flat = cells.reshape(count * HALF, LANES)
-    lane = lax.broadcasted_iota(jnp.int32, flat.shape, 1)
-    x = lane % CELL
-    row = lax.broadcasted_iota(jnp.int32, flat.shape, 0) % HALF
+    flat = cells.reshape(count * CELL, LANES)
+    x = lax.broadcasted_iota(jnp.int32, flat.shape, 1) % CELL
+    y = lax.broadcasted_iota(jnp.int32, flat.shape, 0) % CELL
     before = jnp.where(x == 0, 0.0, pltpu.roll(flat, 1, 1))
     after = jnp.where(x == CELL - 1, 0.0, pltpu.roll(flat, LANES - 1, 1))
-    other = pltpu.roll(flat, CELL, 1)
-    up = jnp.where(row == 0, 0.0, pltpu.roll(other, 1, 0))
-    down = jnp.where(row == HALF - 1, 0.0, pltpu.roll(other, count * HALF - 1, 0))
-    beside = before + after + other + jnp.where(lane < CELL, up, down)
-    return (0.5 * flat + 0.125 * beside).reshape(cells.shape)
+    up = jnp.where(y == 0, 0.0, pltpu.roll(flat, 1, 0))
+    down = jnp.where(y == CELL - 1, 0.0, pltpu.roll(flat, count * CELL - 1, 0))
+    return (0.5 * flat + 0.125 * (before + after + up + down)).reshape(cells.shape)
 
 
 def update_kernel(
@@ -592,28 +629,29 @@
 def per_device(
     masters, inst_master, inst_orient, owner_map, tile_free, target, kernel_spectra, socs_weights
 ):
-    stored = masters.shape[0]
+    stored = masters.shape[0] // 2
     total = owner_map.shape[0]
     consts = tables(TILE + 2 * HALO, kernel_spectra.shape[1], HALO, TILE)
-    rows_place, rows_t, cols_place = placements()
-    own = masters.reshape(stored, HALF, LANES)
+    flip, spread = flips()
+    own = masters.reshape(stored, 2, CELL, CELL).transpose(0, 2, 1, 3).reshape(stored, CELL, LANES)
     n_row = lax.axis_size("row")
     n_col = lax.axis_size("col")
     table = gather_masters(own.astype(jnp.bfloat16), n_row, n_col)
-    shading, mask, edge_l, edge_r = image(
-        inst_master, inst_orient, owner_map, table, tile_free, rows_place, cols_place, True
+    mask, edge_l, edge_r = image(
+        inst_master, inst_orient, owner_map, table, tile_free, flip, spread, True
     )
     padded = with_halo(mask, edge_l, edge_r, n_row, n_col)
     resist, new_free, sums = tile_steps(
-        inst_master, inst_orient, owner_map, socs_weights, padded, target, shading, tile_free,
-        kernel_spectra, consts, rows_t, cols_place, total,
+        inst_master, inst_orient, owner_map, socs_weights, padded, target, tile_free,
+        kernel_spectra, consts, flip, total,
     )
     table = update_masters(sums, own, n_row, n_col)
     fresh = lax.dynamic_slice_in_dim(table, lax.axis_index("col") * stored, stored, 0)
     (new_mask,) = image(
-        inst_master, inst_orient, owner_map, table, new_free, rows_place, cols_place, False
+        inst_master, inst_orient, owner_map, table, new_free, flip, spread, False
     )
-    return (resist, new_mask, fresh.astype(jnp.float32).reshape(masters.shape))
+    fresh = fresh.astype(jnp.float32).reshape(stored, CELL, 2, CELL).transpose(0, 2, 1, 3)
+    return (resist, new_mask, fresh.reshape(masters.shape))
 
 
 def solution(mesh):

time: 182 us -> 152 us (0.84)
  Pallas kernels: 177 us -> 146 us
    pallas_call x1, Pallas kernels: 71.1 us -> 35.4 us  [tile_steps(): pl.pallas_call(tile_kernel, grid_spec=pltpu.PrefetchScalarGridSpec(num_sc...]
    pallas_call x2, Pallas kernels: 30 us -> 35 us  [image(): pl.pallas_call(functools.partial(image_kernel, emit_mask), grid_spec=pltp...]
    reshape x0 -> x6, local copies, waits for them, and re-layouts: none -> 3.11 us  [the longest x3 1.85 us: per_device(): masters.reshape(stored, 2, CELL, CELL).transpose(0, 2, 1, 3)]
    unnamed x4 -> x2, local copies, waits for them, and re-layouts: 1.87 us -> 0.01 us
where the time goes in v1:
time: 152 us; the launch traced here: 151 us
  Pallas kernels  146 us (96%)
  local copies, waits for them, and re-layouts  3.11 us (2%)
  other arithmetic  1.65 us (1%)
    pallas_call x1, Pallas kernels, update_masters(): pl.pallas_call(functools.partial(update_kernel, n_row, n_col), in_specs=[...  44.7 us
    pallas_call x1, Pallas kernels, tile_steps(): pl.pallas_call(tile_kernel, grid_spec=pltpu.PrefetchScalarGridSpec(num_sc...  35.4 us
    pallas_call x2, Pallas kernels, image(): pl.pallas_call(functools.partial(image_kernel, emit_mask), grid_spec=pltp...  35 us
    pallas_call x1, Pallas kernels, gather_masters(): pl.pallas_call(functools.partial(gather_kernel, n_row, n_col), in_specs=[...  17.5 us
    pallas_call x1, Pallas kernels, with_halo(): pl.pallas_call(functools.partial(halo_kernel, n_row, n_col), in_specs=[VM...  13.2 us

profile of v1, /device:TPU:0, one launch (start us, length us, event | category | flops | bytes accessed | tf_op | source)
XLA Modules:
  0.0 151.3 jit_solution(9678987398087688432)
XLA Ops:
  0.6 1.1 reshape.22
  1.8 0.4 copy.26
  2.2 0.3 reshape.23.own_ref
  2.5 0.0 copy-start
  2.5 0.7 convert_element_type.4.own_ref
  3.2 17.5 %gather_masters.1.table_ref = bf16[64,64,128]{2,1,0:T(8,128)(2,1)} custom-call(bf16[8,64,128]{2,1,0:T(8,128)(2,1)} %convert_element_type.4.own_ref), custom_call_target="tpu_custom_call" | custom-call | tf_op jit(solution)/shard_map/gather_masters/pallas_call | solution.py:432
  20.8 17.4 %image.2 = (bf16[1024,1024]{1,0:T(8,128)(2,1)}, bf16[512,128]{1,0:T(8,128)(2,1)}, bf16[512,128]{1,0:T(8,128)(2,1)}) custom-call(s32[16,16]{1,0:T(8,128)} %inst_ref.5, s32[16,16]{1,0:T(8,128)} %orient_ref.5, s32[128]{0:T(128)} %owner_ref.5, bf16[64,64,128]{2,1,0:T(8,128)(2,1)} %gather_masters.1.table_ref, f32[1024,1024]{1,0:T(8,128)} %free_ref.3, ...), custom_call_target="tpu_custom_call" | custom-call | tf_op jit(solution)/shard_map/image/pallas_call | solution.py:147
  38.2 13.2 %with_halo.1.padded_ref = bf16[1152,1280]{1,0:T(8,128)(2,1)} custom-call(bf16[1024,1024]{1,0:T(8,128)(2,1)} %get-tuple-element.9.mask_ref, bf16[512,128]{1,0:T(8,128)(2,1)} %get-tuple-element.10.edge_l_ref, bf16[512,128]{1,0:T(8,128)(2,1)} %get-tuple-element.11.edge_r_ref), custom_call_target="tpu_custom_call" | custom-call | tf_op jit(solution)/shard_map/with_halo/pallas_call | solution.py:519
  51.3 0.0 copy-done
  51.3 35.4 %tile_steps.1 = (f32[1024,1024]{1,0:T(8,128)}, f32[1024,1024]{1,0:T(8,128)}, bf16[64,64,128]{2,1,0:T(8,128)(2,1)}) custom-call(s32[16,16]{1,0:T(8,128)} %inst_ref.5, s32[16,16]{1,0:T(8,128)} %orient_ref.5, s32[128]{0:T(128)} %owner_ref.5, f32[8]{0:T(128)} %weights_ref.1, bf16[1152,1280]{1,0:T(8,128)(2,1)} %with_halo.1.padded_ref, f32[1024,1024]{1,0:T(8,128)} %target_ref.1, ...), custom_call_target="tpu_custom_call" | custom-call | tf_op jit(solution)/shard_map/tile_steps/pallas_call | solution.py:295
  86.8 44.7 %update_masters.1.table_ref = bf16[64,64,128]{2,1,0:T(8,128)(2,1)} custom-call(bf16[64,64,128]{2,1,0:T(8,128)(2,1)} %get-tuple-element.13.sums_ref, f32[8,64,128]{2,1,0:T(8,128)} %copy-done), custom_call_target="tpu_custom_call" | custom-call | tf_op jit(solution)/shard_map/update_masters/pallas_call | solution.py:612
  131.5 17.6 %image.3 = f32[1024,1024]{1,0:T(8,128)} custom-call(s32[16,16]{1,0:T(8,128)} %inst_ref.5, s32[16,16]{1,0:T(8,128)} %orient_ref.5, s32[128]{0:T(128)} %owner_ref.5, bf16[64,64,128]{2,1,0:T(8,128)(2,1)} %update_masters.1.table_ref, f32[1024,1024]{1,0:T(8,128)} %get-tuple-element.14.free_ref, bf16[256,256]{1,0:T(8,128)(2,1)} %constant.44.clone.flip_ref, ...), custom_call_target="tpu_custom_call" | custom-call | tf_op jit(solution)/shard_map/image/pallas_call | solution.py:147
  149.1 0.9 dynamic-slice_convert_fusion
  150.0 0.3 reshape.31
  150.4 0.9 reshape.28
  (1 shorter events, 0.0 us)
Async XLA Ops:
  2.5 48.8 %copy-start = (f32[8,64,128]{2,1,0:T(8,128)}, f32[8,64,128]{2,1,0:T(8,128)S(1)}, u32[]{:S(2)}) copy-start(f32[8,64,128]{2,1,0:T(8,128)S(1)} %reshape.23.own_ref) | copy-start | bytes 786436

commit v2 on v1

v2 whole, which is shorter than its diff:
```python
import functools
import math

import jax
import jax.numpy as jnp
import numpy as np
from jax import lax
from jax.experimental import pallas as pl
from jax.experimental.pallas import tpu as pltpu
from jax.sharding import PartitionSpec as P

TILE = 512
TPD = 2
HALO = 64
CELL = 64
LANES = 128
HALF = CELL // 2
STRIP = 16
GROUP = 4
SLAB = 256
VM = pl.BlockSpec(memory_space=pltpu.VMEM)
MESH = pl.DeviceIdType.MESH
GAIN_GRID = 1.9925
GAIN_SPREAD = 1.725625

step_free = 1.0
step_master = 0.05
resist_gain = 2.0
resist_level = 1.8


def dot(left, right):
    return jnp.dot(left, right, preferred_element_type=jnp.float32)


def bfloat(value):
    return jnp.asarray(np.ascontiguousarray(value).astype(jnp.bfloat16))


def tables(pad_side, band_side, halo, tile):
    freqs = np.arange(band_side, dtype=np.int64) - band_side // 2
    phases = (freqs[:, None] * np.arange(pad_side)[None, :]) % pad_side
    angles = phases.astype(np.float32) * np.float32(2.0 * math.pi / pad_side)
    cos = np.cos(angles)
    sin = np.sin(angles)
    cos_in = cos[:, halo : halo + tile]
    sin_in = sin[:, halo : halo + tile]
    cs_full = np.concatenate([cos, sin], 0)
    cs_lanes = np.pad(cs_full, ((0, 0), (LANES - halo, LANES - halo)))
    cs_in = np.concatenate([cos_in, sin_in], 0)
    grid = 2 * band_side
    turns = (freqs[:, None] * np.arange(grid)[None, :]) % grid
    cos_g = GAIN_GRID * np.cos(turns * (2.0 * math.pi / grid))
    sin_g = GAIN_GRID * np.sin(turns * (2.0 * math.pi / grid))
    cs_g = np.concatenate([cos_g, sin_g], 0)
    field = np.block([[cos_g, sin_g], [-sin_g, cos_g]])
    gaps = np.arange(halo, halo + tile)[:, None] / pad_side - np.arange(grid)[None, :] / grid
    waves = np.arange(1, band_side)
    spread = (1.0 + 2.0 * np.cos(2.0 * math.pi * gaps[:, :, None] * waves).sum(-1)) * (GAIN_SPREAD / grid)
    parts = (cs_full, cs_lanes.T, cs_g, cs_g.T, field, field.T, spread, spread.T, cs_in, cs_in.T)
    return [bfloat(p) for p in parts]


def flips():
    back = np.eye(CELL)[::-1]
    rows = np.kron(np.eye(4), back)
    same = np.eye(CELL)
    none = np.zeros((CELL, CELL))
    spread = [
        np.block([[m, m], [none, none]]) if e == 0 else np.block([[none, none], [m, m]])
        for m in (same, back)
        for e in range(2)
    ]
    return bfloat(rows), bfloat(np.concatenate(spread, 1))


def left_mask(rows):
    return lax.broadcasted_iota(jnp.int32, (rows, LANES), 1) < CELL


def pair_codes(inst_ref, orient_ref, owner_ref, a, b):
    s0 = owner_ref[inst_ref[a, b]]
    s1 = owner_ref[inst_ref[a, b + 1]]
    return s0, s1, orient_ref[a, b], orient_ref[a, b + 1]


def turn_block(table_ref, turned_ref, flip_ref, spread_ref, at, count):
    total = turned_ref.shape[0] // 4
    rows = count * CELL
    cells = table_ref[pl.ds(at, count)].reshape(rows, LANES)
    flipped = dot(flip_ref[:rows, :rows], cells).astype(jnp.bfloat16)
    both = dot(jnp.concatenate([cells, flipped], axis=0), spread_ref[...]).astype(jnp.bfloat16)
    for f in range(2):
        for c in range(2):
            for e in range(2):
                lanes = slice((2 * c + e) * LANES, (2 * c + e + 1) * LANES)
                for p in range(count):
                    start = f * rows + p * CELL
                    turned_ref[(2 * c + f) * total + 2 * (at + p) + e] = both[start : start + CELL, lanes]


def assemble_pair(turned_ref, codes):
    s0, s1, o0, o1 = codes
    total = turned_ref.shape[0] // 4
    one = turned_ref[o0 * total + s0].astype(jnp.float32)
    two = turned_ref[o1 * total + s1].astype(jnp.float32)
    return jnp.where(left_mask(CELL), one, two)


def image_kernel(inst_ref, orient_ref, owner_ref, turned_ref, free_ref, out_ref):
    steps = free_ref.shape[0] // CELL
    first = pl.program_id(0) * steps

    def step(a, carry):
        rows = pl.ds(pl.multiple_of(a * CELL, CELL), CELL)
        for pair in range(free_ref.shape[1] // LANES):
            codes = pair_codes(inst_ref, orient_ref, owner_ref, first + a, 2 * pair)
            cells = assemble_pair(turned_ref, codes)
            lanes = slice(pair * LANES, (pair + 1) * LANES)
            out_ref[rows, lanes] = jnp.tanh(cells + free_ref[rows, lanes])
        return carry

    lax.fori_loop(0, steps, step, 0)


def whole_spec(array):
    zeros = (0,) * array.ndim
    return pl.BlockSpec(array.shape, lambda *_: zeros)


def image(inst, orient, owner, turned, free):
    height, width = free.shape
    strip = pl.BlockSpec((SLAB, width), lambda a, *_: (a, 0))
    return pl.pallas_call(
        image_kernel,
        grid_spec=pltpu.PrefetchScalarGridSpec(
            num_scalar_prefetch=3,
            grid=(height // SLAB,),
            in_specs=[VM, strip],
            out_specs=strip,
        ),
        out_shape=jax.ShapeDtypeStruct(free.shape, jnp.float32),
        compiler_params=pltpu.CompilerParams(vmem_limit_bytes=8 * 1024 * 1024),
        name="image",
    )(inst, orient, owner, turned, free)


def tile_kernel(
    n_row, n_col, inst_ref, orient_ref, owner_ref, weights_ref,
    padded_ref, target_ref, free_ref, spectra_ref,
    cs_full_ref, cs_lanes_t_ref, cs_g_ref, cs_g_t_ref, field_ref, field_t_ref,
    spread_ref, spread_t_ref, cs_in_ref, cs_in_t_ref, flip_ref,
    resist_ref, new_free_ref, sums_ref,
    kern_s, half_s, field_s, bhalf_s, level_s, turned_s, sums_s,
):
    i = pl.program_id(0)
    j = pl.program_id(1)
    band = spectra_ref.shape[1]
    kernels = spectra_ref.shape[2]
    tile = target_ref.shape[0]
    pad_side = cs_full_ref.shape[1]
    pad_lanes = cs_lanes_t_ref.shape[0]
    grid = 2 * band
    blocks = grid // STRIP
    low = lambda v: v.astype(jnp.bfloat16)

    @pl.when((i == 0) & (j == 0))
    def _():
        sums_s[...] = jnp.zeros_like(sums_s)
        for k in range(kernels):
            weight = jnp.full((band, LANES), weights_ref[k], jnp.float32)
            scale = jnp.sqrt(weight) / (pad_side * band * GAIN_GRID**2)
            for part in range(2):
                kern_s[part, k] = spectra_ref[part, :, k, :] * scale

    at_row = i * tile
    at_col = j * tile
    window = padded_ref[
        pl.ds(pl.multiple_of(at_row, 128), pad_side), pl.ds(pl.multiple_of(at_col, 128), pad_lanes)
    ]
    forw = low(dot(cs_full_ref[...], window))
    spec = dot(forw, cs_lanes_t_ref[...])
    spec_re = spec[:band, :band] + spec[band:, band:]
    spec_im = spec[band:, :band] - spec[:band, band:]
    for k in range(kernels):
        amp_re = low(kern_s[0, k] * spec_re - kern_s[1, k] * spec_im)
        amp_im = low(kern_s[0, k] * spec_im + kern_s[1, k] * spec_re)
        upper = jnp.concatenate([amp_re, amp_im], axis=1)
        lower = jnp.concatenate([-amp_im, amp_re], axis=1)
        half = low(dot(cs_g_t_ref[...], jnp.concatenate([upper, lower], axis=0)))
        half_s[:, k] = half.reshape(blocks, STRIP, grid)
    for b in range(0, blocks, GROUP):
        lines = half_s[b : b + GROUP].reshape(GROUP * kernels * STRIP, grid)
        field = dot(lines, field_ref[...])
        re = field[:, :grid]
        im = field[:, grid:]
        power = (re * re + im * im).reshape(GROUP, kernels, STRIP, grid)
        level_s[b : b + GROUP] = jnp.sum(power, axis=1)
        field_s[b : b + GROUP] = low(field).reshape(GROUP, kernels, STRIP, 2 * grid)
    level = level_s[...].reshape(grid, grid)
    mean = jnp.sum(jnp.sum(level, axis=0, keepdims=True), axis=1, keepdims=True) / (grid * grid)
    lines = low(dot(spread_ref[...], low(level - mean)))
    intensity = dot(lines, spread_t_ref[...]) * (1.0 / GAIN_SPREAD**2) + mean
    resist = jax.nn.sigmoid(resist_gain * (intensity - resist_level))
    resist_ref[...] = resist
    slopes = (4.0 * resist_gain / GAIN_SPREAD**2) * (resist - target_ref[...]) * resist * (1.0 - resist)
    lines = low(dot(spread_t_ref[...], low(slopes)))
    level_s[...] = dot(lines, spread_ref[...]).reshape(blocks, STRIP, grid)
    for b in range(0, blocks, GROUP):
        pull = level_s[b : b + GROUP].reshape(GROUP, 1, STRIP, grid)
        pull = jnp.concatenate([pull, pull], axis=3)
        back = low(field_s[b : b + GROUP].astype(jnp.float32) * pull)
        bhalf = low(dot(back.reshape(GROUP * kernels * STRIP, 2 * grid), field_t_ref[...]))
        bhalf = bhalf.reshape(GROUP, kernels, STRIP, grid)
        for g in range(GROUP):
            bhalf_s[:, b + g] = bhalf[g]
    bspec_re = jnp.zeros((band, band), jnp.float32)
    bspec_im = jnp.zeros((band, band), jnp.float32)
    for k in range(kernels):
        bamp = dot(cs_g_ref[...], bhalf_s[k].reshape(grid, grid))
        bamp_re = bamp[:band, :band] + bamp[band:, band:]
        bamp_im = bamp[:band, band:] - bamp[band:, :band]
        bspec_re += kern_s[0, k] * bamp_re + kern_s[1, k] * bamp_im
        bspec_im += kern_s[0, k] * bamp_im - kern_s[1, k] * bamp_re
    upper = jnp.concatenate([low(bspec_re), low(-bspec_im)], axis=1)
    lower = jnp.concatenate([low(bspec_im), low(bspec_re)], axis=1)
    bforw = low(dot(jnp.concatenate([upper, lower], axis=0), cs_in_ref[...]))
    gradient = dot(cs_in_t_ref[...], bforw)
    shading = padded_ref[
        pl.ds(pl.multiple_of(at_row + HALO, HALO), tile), pl.ds(pl.multiple_of(at_col + LANES, LANES), tile)
    ].astype(jnp.float32)
    grad_param = gradient * (1.0 - shading * shading)
    new_free_ref[...] = free_ref[...] - step_free * grad_param
    turned_s[0] = grad_param
    plain = low(grad_param)
    group = flip_ref.shape[0]
    for at in range(0, tile, group):
        part = slice(at, at + group)
        across = dot(plain[:, part], flip_ref[...])
        turned_s[2, :, part] = across
        for f, source in ((1, plain[:, part]), (3, low(across))):
            for up in range(0, tile, group):
                turned_s[f, up : up + group, part] = dot(flip_ref[...], source[up : up + group])
    cells = tile // CELL
    left = left_mask(CELL)

    def cells_step(a, carry):
        rows = pl.ds(pl.multiple_of(a * CELL, CELL), CELL)
        for pair in range(cells // 2):
            s0, s1, o0, o1 = pair_codes(
                inst_ref, orient_ref, owner_ref, i * cells + a, j * cells + 2 * pair
            )
            lanes = slice(pair * LANES, (pair + 1) * LANES)
            sums_s[s0] += jnp.where(left, turned_s[o0, rows, lanes], 0.0)
            sums_s[s1] += jnp.where(left, 0.0, turned_s[o1, rows, lanes])
        return carry

    lax.fori_loop(0, cells, cells_step, 0)

    @pl.when((i == pl.num_programs(0) - 1) & (j == pl.num_programs(1) - 1))
    def _():
        stored = sums_ref.shape[0] // n_col
        share = stored // n_row

        def pack(p, carry):
            one = sums_s[2 * p]
            two = sums_s[2 * p + 1]
            one = one + pltpu.roll(one, CELL, 1)
            two = two + pltpu.roll(two, CELL, 1)
            col = p // stored
            row = p % stored // share
            side = row % 2 * (n_col // 2) + col // 2
            spot = (side * n_row + row // 2 * 2 + col % 2) * share + p % share
            sums_ref[spot] = low(jnp.where(left, one, two))
            return carry

        lax.fori_loop(0, sums_ref.shape[0], pack, 0)


def tile_steps(inst, orient, owner, weights, padded, target, free, spectra, consts, flip, masters, n_row, n_col):
    height, width = target.shape
    band = spectra.shape[1]
    kernels = spectra.shape[2]
    grid = 2 * band
    blocks = grid // STRIP
    tile_spec = pl.BlockSpec((TILE, TILE), lambda i, j, *_: (i, j))
    sums_shape = (masters // 2, CELL, LANES)
    once = [padded, None, None, spectra, *consts, flip]
    return pl.pallas_call(
        functools.partial(tile_kernel, n_row, n_col),
        grid_spec=pltpu.PrefetchScalarGridSpec(
            num_scalar_prefetch=4,
            grid=(height // TILE, width // TILE),
            in_specs=[tile_spec if v is None else whole_spec(v) for v in once],
            out_specs=[tile_spec, tile_spec, pl.BlockSpec(sums_shape, lambda *_: (0, 0, 0))],
            scratch_shapes=[
                pltpu.VMEM((2, kernels, band, band), jnp.float32),
                pltpu.VMEM((blocks, kernels, STRIP, grid), jnp.bfloat16),
                pltpu.VMEM((blocks, kernels, STRIP, 2 * grid), jnp.bfloat16),
                pltpu.VMEM((kernels, blocks, STRIP, grid), jnp.bfloat16),
                pltpu.VMEM((blocks, STRIP, grid), jnp.float32),
                pltpu.VMEM((4, TILE, TILE), jnp.float32),
                pltpu.VMEM((masters, CELL, LANES), jnp.float32),
            ],
        ),
        out_shape=[
            jax.ShapeDtypeStruct(target.shape, jnp.float32),
            jax.ShapeDtypeStruct(target.shape, jnp.float32),
            jax.ShapeDtypeStruct(sums_shape, jnp.bfloat16),
        ],
        compiler_params=pltpu.CompilerParams(vmem_limit_bytes=60 * 1024 * 1024),
        name="tile_steps",
    )(inst, orient, owner, weights, padded, target, free, spectra, *consts, flip)


def greet(peers):
    barrier = pltpu.get_barrier_semaphore()
    for peer in peers:
        pl.semaphore_signal(barrier, inc=1, device_id=peer, device_id_type=MESH)
    pl.semaphore_wait(barrier, len(peers))


def level_peers(n_row, n_col):
    r = lax.axis_index("row")
    c = lax.axis_index("col")
    long = n_col // 2
    z, y = lax.div(c, 2), lax.rem(c, 2)
    x, core = lax.div(r, 2), lax.rem(r, 2)
    p = x * 2 + y

    def z_at(t):
        return lax.rem(z + t + long, long)

    def p_at(t):
        q = lax.rem(p + t + n_row, n_row)
        return lax.div(q, 2), lax.rem(q, 2)

    return r, c, z, y, x, core, long, z_at, p_at


def gather_ids(n_row, n_col):
    r, c, z, y, x, core, long, z_at, p_at = level_peers(n_row, n_col)
    ids = [(r, z_at(t) * 2 + y) for t in range(1, long)]
    for t in range(1, n_row):
        px, py = p_at(t)
        ids.append((px * 2 + core, z * 2 + py))
    return ids + [(x * 2 + 1 - core, c)]


def gather_levels(n_row, n_col, own, table_ref, stored, send_sem, recv_sem, ready):
    r, c, z, y, x, core, long, z_at, p_at = level_peers(n_row, n_col)
    share = stored // n_row
    partner = (x * 2 + 1 - core, c)

    def first_row(row, col):
        return col * stored + row * share

    def make(src, at, level, slot, peer):
        return pltpu.make_async_remote_copy(
            src_ref=src,
            dst_ref=table_ref.at[pl.ds(at, share)],
            send_sem=send_sem.at[level, slot],
            recv_sem=recv_sem.at[level, slot],
            device_id=peer,
            device_id_type=MESH,
        )

    def here(at):
        return table_ref.at[pl.ds(at, share)]

    mine = first_row(r, c)
    first = [make(own, mine, 0, t, (r, z_at(t) * 2 + y)) for t in range(1, long)]
    for copy in first:
        copy.start()
    second = []
    third = []
    for t in range(long):
        if t > 0:
            first[t - 1].wait_recv()
        at = first_row(r, z_at(-t) * 2 + y)
        src = own if t == 0 else here(at)
        for q in range(1, n_row):
            px, py = p_at(q)
            copy = make(src, at, 1, t * n_row + q, (px * 2 + core, z * 2 + py))
            copy.start()
            second.append(copy)
        copy = make(src, at, 2, t * n_row, partner)
        copy.start()
        third.append(copy)
    for t in range(long):
        ready(first_row(r, z_at(-t) * 2 + y))

    def across(n, carry):
        t = n // (n_row - 1)
        q = n % (n_row - 1) + 1
        slot = t * n_row + q
        px, py = p_at(-q)
        at = first_row(px * 2 + core, z_at(-t) * 2 + py)
        make(here(at), at, 1, slot, partner).wait_recv()
        make(here(at), at, 2, slot, partner).start()
        ready(at)
        return carry

    def beside(n, carry):
        t = n // n_row
        q = n % n_row
        px, py = p_at(-q)
        at = first_row(px * 2 + 1 - core, z_at(-t) * 2 + py)
        make(here(at), at, 2, n, partner).wait_recv()
        ready(at)
        return carry

    def sent(n, carry):
        make(here(mine), mine, 2, n, partner).wait_send()
        return carry

    lax.fori_loop(0, long * (n_row - 1), across, 0)
    lax.fori_loop(0, long * n_row, beside, 0)
    for copy in first + second:
        copy.wait_send()
    lax.fori_loop(0, long * n_row, sent, 0)


def gather_sems(n_row, n_col):
    shape = (3, n_row * n_col // 2)
    return [pltpu.SemaphoreType.DMA(shape), pltpu.SemaphoreType.DMA(shape)]


def front_kernel(
    n_row, n_col, inst_ref, orient_ref, owner_ref, own_ref, free_ref, flip_ref, spread_ref, out_ref,
    table_s, turned_s, free_s, edge_l, edge_r, from_l, from_r,
    free_sem, send_sem, recv_sem, halo_send, halo_recv,
):
    r = lax.axis_index("row")
    c = lax.axis_index("col")
    height, width = free_s.shape
    packed = height // 2
    stored = own_ref.shape[0]
    share = stored // n_row
    load_free = pltpu.make_async_copy(free_ref, free_s, free_sem)
    load_free.start()
    moves = [(0, 1), (0, -1), (1, 0), (-1, 0), (1, 1), (1, -1), (-1, 1), (-1, -1)]
    ids = [(lax.rem(r + n_row + dr, n_row), lax.rem(c + n_col + dc, n_col)) for dr, dc in moves]
    greet(gather_ids(n_row, n_col) + ids)
    own = own_ref.at[pl.ds(r * share, share)]
    table_s[pl.ds(c * stored + r * share, share)] = own_ref[pl.ds(r * share, share)]

    def ready(at):
        turn_block(table_s, turned_s, flip_ref, spread_ref, at, share)

    gather_levels(n_row, n_col, own, table_s, stored, send_sem, recv_sem, ready)
    load_free.wait()

    pairs = width // LANES
    strips = height // CELL
    cast = lambda v: v.astype(jnp.bfloat16)
    left = left_mask(HALF)

    def draw(a, pair):
        codes = pair_codes(inst_ref, orient_ref, owner_ref, a, 2 * pair)
        cells = assemble_pair(turned_s, codes)
        rows = pl.ds(pl.multiple_of(a * CELL, CELL), CELL)
        value = jnp.tanh(cells + free_s[rows, pair * LANES : (pair + 1) * LANES])
        rows = pl.ds(pl.multiple_of(HALO + a * CELL, CELL), CELL)
        out_ref[rows, (pair + 1) * LANES : (pair + 2) * LANES] = cast(value)
        return value

    def outer(n, carry):
        for pair in range(1, pairs - 1):
            draw(n * (strips - 1), pair)
        return carry

    def sides(a, carry):
        rows = pl.ds(pl.multiple_of(a * HALF, HALF), HALF)
        value = draw(a, 0)
        edge_l[rows] = cast(jnp.where(left, value[:HALF], pltpu.roll(value[HALF:], CELL, 1)))
        value = draw(a, pairs - 1)
        edge_r[rows] = cast(jnp.where(left, pltpu.roll(value[:HALF], CELL, 1), value[HALF:]))
        return carry

    def inner(a, carry):
        for pair in range(1, pairs - 1):
            draw(a, pair)
        return carry

    lax.fori_loop(0, 2, outer, 0)
    lax.fori_loop(0, strips, sides, 0)
    lax.fori_loop(1, 3, inner, 0)

    middle = slice(LANES, LANES + width)
    row_parts = {
        -1: (slice(HALO, 2 * HALO), slice(HALO + height, 2 * HALO + height)),
        1: (slice(height, HALO + height), slice(0, HALO)),
    }
    edge_parts = {
        -1: (slice(0, HALF), slice(HALF + packed, 2 * HALF + packed)),
        0: (slice(0, packed), slice(HALF, HALF + packed)),
        1: (slice(packed - HALF, packed), slice(0, HALF)),
    }

    def inside(dr, dc):
        return (r + dr >= 0) & (r + dr < n_row) & (c + dc >= 0) & (c + dc < n_col)

    work = []
    for at, (dr, dc) in enumerate(moves):
        if dc == 0:
            src, dst = row_parts[dr]
            src, dst = out_ref.at[src, middle], out_ref.at[dst, middle]
        else:
            src, dst = edge_parts[dr]
            src = (edge_r if dc == 1 else edge_l).at[src]
            dst = (from_l if dc == 1 else from_r).at[dst]
        copy = pltpu.make_async_remote_copy(
            src_ref=src,
            dst_ref=dst,
            send_sem=halo_send.at[at],
            recv_sem=halo_recv.at[at],
            device_id=ids[at],
            device_id_type=MESH,
        )
        work.append((copy, dst, inside(dr, dc), inside(-dr, -dc)))
    for copy, dst, sends, gets in work:
        pl.when(sends)(copy.start)
    lax.fori_loop(3, strips - 1, inner, 0)
    for copy, dst, sends, gets in work:

        @pl.when(jnp.logical_not(gets))
        def _():
            dst[...] = jnp.zeros(dst.shape, dst.dtype)

    for copy, dst, sends, gets in work:
        pl.when(gets)(copy.wait_recv)

    def unpack(a, carry):
        rows = pl.ds(pl.multiple_of(a * HALF, HALF), HALF)
        upper = pl.ds(pl.multiple_of(a * CELL, CELL), HALF)
        lower = pl.ds(pl.multiple_of(a * CELL + HALF, HALF), HALF)
        one = from_l[rows].astype(jnp.float32)
        two = from_r[rows].astype(jnp.float32)
        last = slice(LANES + width, 2 * LANES + width)
        out_ref[upper, :LANES] = cast(jnp.where(left, 0.0, pltpu.roll(one, CELL, 1)))
        out_ref[lower, :LANES] = cast(jnp.where(left, 0.0, one))
        out_ref[upper, last] = cast(jnp.where(left, two, 0.0))
        out_ref[lower, last] = cast(jnp.where(left, pltpu.roll(two, CELL, 1), 0.0))
        return carry

    lax.fori_loop(0, (height + 2 * HALO) // CELL, unpack, 0)
    for copy, dst, sends, gets in work:
        pl.when(sends)(copy.wait_send)


def front(inst, orient, owner, own, free, flip, spread, n_row, n_col):
    height, width = free.shape
    smem = pl.BlockSpec(memory_space=pltpu.SMEM)
    low = jnp.bfloat16
    pairs = n_col * own.shape[0]
    return pl.pallas_call(
        functools.partial(front_kernel, n_row, n_col),
        in_specs=[smem, smem, smem, VM, pl.BlockSpec(memory_space=pl.ANY), VM, VM],
        out_specs=VM,
        out_shape=jax.ShapeDtypeStruct((height + 2 * HALO, width + 2 * LANES), low),
        scratch_shapes=[
            pltpu.VMEM((pairs, CELL, LANES), low),
            pltpu.VMEM((8 * pairs, CELL, LANES), low),
            pltpu.VMEM((height, width), jnp.float32),
            pltpu.VMEM((height // 2, LANES), low),
            pltpu.VMEM((height // 2, LANES), low),
            pltpu.VMEM((height // 2 + 2 * HALF, LANES), low),
            pltpu.VMEM((height // 2 + 2 * HALF, LANES), low),
            pltpu.SemaphoreType.DMA,
            *gather_sems(n_row, n_col),
            pltpu.SemaphoreType.DMA((8,)),
            pltpu.SemaphoreType.DMA((8,)),
        ],
        compiler_params=pltpu.CompilerParams(
            collective_id=0, has_side_effects=True, vmem_limit_bytes=40 * 1024 * 1024
        ),
        name="front",
    )(inst, orient, owner, own, free, flip, spread)


def smooth_packed(cells):
    count = cells.shape[0]
    flat = cells.reshape(count * CELL, LANES)
    x = lax.broadcasted_iota(jnp.int32, flat.shape, 1) % CELL
    y = lax.broadcasted_iota(jnp.int32, flat.shape, 0) % CELL
    before = jnp.where(x == 0, 0.0, pltpu.roll(flat, 1, 1))
    after = jnp.where(x == CELL - 1, 0.0, pltpu.roll(flat, LANES - 1, 1))
    up = jnp.where(y == 0, 0.0, pltpu.roll(flat, 1, 0))
    down = jnp.where(y == CELL - 1, 0.0, pltpu.roll(flat, count * CELL - 1, 0))
    return (0.5 * flat + 0.125 * (before + after + up + down)).reshape(cells.shape)


def update_kernel(
    n_row, n_col, sums_ref, own_ref, flip_ref, spread_ref, turned_ref, fresh_ref,
    table_s, fresh, rc, mid, rp, zb, rz,
    core_send, core_recv, p_send, p_recv, z_send, z_recv, send_sem, recv_sem,
):
    r, c, z, y, x, core, long, z_at, p_at = level_peers(n_row, n_col)
    p = x * 2 + y
    stored = own_ref.shape[0]
    share = stored // n_row
    low = lambda v: v.astype(jnp.bfloat16)
    high = lambda v: v.astype(jnp.float32)
    greet(gather_ids(n_row, n_col))
    order = [*range(1, long), 0]

    def make(src, dst, send, recv, at, peer):
        return pltpu.make_async_remote_copy(
            src_ref=src,
            dst_ref=dst,
            send_sem=send.at[at],
            recv_sem=recv.at[at],
            device_id=peer,
            device_id_type=MESH,
        )

    def chunk(side, t):
        return pl.ds((side * long + z_at(t)) * stored, stored)

    to_core = {}
    for t in order:
        src = sums_ref.at[chunk(1 - core, t)]
        to_core[t] = make(src, rc.at[t], core_send, core_recv, t, (x * 2 + 1 - core, c))
        to_core[t].start()
    to_p = {}
    for t in order:
        to_core[t].wait_recv()
        mid[t] = low(high(sums_ref[chunk(core, t)]) + high(rc[t]))
        for q in range(1, n_row):
            px, py = p_at(q)
            src = mid.at[t, pl.ds((px * 2 + py) * share, share)]
            at = t * n_row + q
            to_p[at] = make(src, rp.at[at], p_send, p_recv, at, (px * 2 + core, z * 2 + py))
            to_p[at].start()
    to_z = {}
    for t in order:
        total = high(mid[t, pl.ds(p * share, share)])
        for q in range(1, n_row):
            at = t * n_row + q
            to_p[at].wait_recv()
            total = total + high(rp[at])
        if t > 0:
            zb[t] = low(total)
            to_z[t] = make(zb.at[t], rz.at[t], z_send, z_recv, t, (r, z_at(t) * 2 + y))
            to_z[t].start()
    for t in range(1, long):
        to_z[t].wait_recv()
        total = total + high(rz[t])
    updated = own_ref[pl.ds(r * share, share)] - step_master * total
    value = low(smooth_packed(updated))
    fresh[...] = value
    table_s[pl.ds(c * stored + r * share, share)] = value

    def ready(at):
        turn_block(table_s, turned_ref, flip_ref, spread_ref, at, share)

    gather_levels(n_row, n_col, fresh, table_s, stored, send_sem, recv_sem, ready)
    fresh_ref[...] = high(table_s[pl.ds(c * stored, stored)])
    for copy in [*to_core.values(), *to_p.values(), *to_z.values()]:
        copy.wait_send()


def update_masters(sums, own, flip, spread, n_row, n_col):
    stored = own.shape[0]
    long = n_col // 2
    share = stored // n_row
    low = jnp.bfloat16
    cells = (CELL, LANES)
    sems = [pltpu.SemaphoreType.DMA((n,)) for n in (long, long, long * n_row, long * n_row, long, long)]
    return pl.pallas_call(
        functools.partial(update_kernel, n_row, n_col),
        in_specs=[VM, VM, VM, VM],
        out_specs=[VM, VM],
        out_shape=[
            jax.ShapeDtypeStruct((8 * sums.shape[0],) + cells, low),
            jax.ShapeDtypeStruct(own.shape, jnp.float32),
        ],
        scratch_shapes=[
            pltpu.VMEM(sums.shape, low),
            pltpu.VMEM((share,) + cells, low),
            pltpu.VMEM((long, stored) + cells, low),
            pltpu.VMEM((long, stored) + cells, low),
            pltpu.VMEM((long * n_row, share) + cells, low),
            pltpu.VMEM((long, share) + cells, low),
            pltpu.VMEM((long, share) + cells, low),
            *sems,
            *gather_sems(n_row, n_col),
        ],
        compiler_params=pltpu.CompilerParams(
            collective_id=2, has_side_effects=True, vmem_limit_bytes=32 * 1024 * 1024
        ),
        name="update_masters",
    )(sums, own, flip, spread)


def per_device(
    masters, inst_master, inst_orient, owner_map, tile_free, target, kernel_spectra, socs_weights
):
    stored = masters.shape[0] // 2
    total = owner_map.shape[0]
    consts = tables(TILE + 2 * HALO, kernel_spectra.shape[1], HALO, TILE)
    flip, spread = flips()
    own = masters.reshape(stored, 2, CELL, CELL).transpose(0, 2, 1, 3).reshape(stored, CELL, LANES)
    n_row = lax.axis_size("row")
    n_col = lax.axis_size("col")
    padded = front(
        inst_master, inst_orient, owner_map, own.astype(jnp.bfloat16), tile_free, flip, spread,
        n_row, n_col,
    )
    resist, new_free, sums = tile_steps(
        inst_master, inst_orient, owner_map, socs_weights, padded, target, tile_free,
        kernel_spectra, consts, flip, total, n_row, n_col,
    )
    turned, fresh = update_masters(sums, own, flip, spread, n_row, n_col)
    new_mask = image(inst_master, inst_orient, owner_map, turned, new_free)
    fresh = fresh.reshape(stored, CELL, 2, CELL).transpose(0, 2, 1, 3)
    return (resist, new_mask, fresh.reshape(masters.shape))


def solution(mesh):
    in_specs = (
        P("col", None),
        P("row", "col"),
        P("row", "col"),
        P(),
        P("row", "col"),
        P("row", "col"),
        P(),
        P(),
    )
    out_specs = (P("row", "col"), P("row", "col"), P("col", None))
    return jax.shard_map(
        per_device, mesh=mesh, in_specs=in_specs, out_specs=out_specs, check_vma=False
    )
```

time: 152 us -> 119 us (0.78)
  Pallas kernels: 146 us -> 103 us
  local copies, waits for them, and re-layouts: 3.11 us -> 14.1 us
  other arithmetic: 1.65 us -> 0.02 us
    pallas_call x5 -> x3, Pallas kernels: 101 us -> 69.6 us  [the longest x1 35.5 us: tile_steps(): pl.pallas_call(functools.partial(tile_kernel, n_row, n_col), grid_spec=pl...]
    unnamed x2 -> x28, local copies, waits for them, and re-layouts: 0.01 us -> 11 us
    pallas_call x1, Pallas kernels: 44.7 us -> 33.7 us  [update_masters(): pl.pallas_call(functools.partial(update_kernel, n_row, n_col), in_specs=[...]
where the time goes in v2:
time: 119 us; the launch traced here: 118 us
  Pallas kernels  103 us (87%)
  local copies, waits for them, and re-layouts  14.1 us (12%)
    pallas_call x1, Pallas kernels, tile_steps(): pl.pallas_call(functools.partial(tile_kernel, n_row, n_col), grid_spec=pl...  35.5 us
    pallas_call x1, Pallas kernels, update_masters(): pl.pallas_call(functools.partial(update_kernel, n_row, n_col), in_specs=[...  33.7 us
    pallas_call x1, Pallas kernels, front(): pl.pallas_call(functools.partial(front_kernel, n_row, n_col), in_specs=[s...  30.4 us
    unnamed x28, local copies, waits for them, and re-layouts  11 us
    pallas_call x1, Pallas kernels, image(): pl.pallas_call(image_kernel, grid_spec=pltpu.PrefetchScalarGridSpec(num_s...  3.6 us

profile of v2, /device:TPU:0, one launch (start us, length us, event | category | flops | bytes accessed | tf_op | source)
XLA Modules:
  0.0 118.2 jit_solution(12149663177490812725)
XLA Ops:
  0.6 1.1 reshape.18
  1.8 0.4 copy.26
  2.2 0.3 reshape.19.own_ref
  2.5 0.0 copy-start
  2.5 2.2 %copy-done = f32[1024,1024]{1,0:T(8,128)S(1)} copy-done((f32[1024,1024]{1,0:T(8,128)S(1)}, f32[1024,1024]{1,0:T(8,128)}, u32[]{:S(2)}) %copy-start) | copy-done | bytes 4194328
  4.7 0.0 copy-start.3
  4.7 0.9 copy-done.3
  5.6 0.0 copy-start.6
  5.6 0.9 copy-done.6
  6.5 0.0 copy-start.8
  6.5 0.7 copy-done.8
  7.2 0.0 copy-start.10
  7.2 0.7 copy-done.10
  7.9 0.0 copy-start.12
  7.9 0.7 copy-done.12
  8.6 30.4 %front.1.padded_ref = bf16[1152,1280]{1,0:T(8,128)(2,1)S(1)} custom-call(s32[16,16]{1,0:T(8,128)S(1)} %copy-done.8, s32[16,16]{1,0:T(8,128)S(1)} %copy-done.10, s32[128]{0:T(128)S(1)} %copy-done.12, bf16[8,64,128]{2,1,0:T(8,128)(2,1)S(1)} %convert_element_type.3.own_ref, f32[1024,1024]{1,0:T(8,128)S(1)} %copy-done, bf16[256,256]{1,0:T(8,128)(2,1)S(1)} %copy-done.3, ...), custom_call_target="tpu_custom_call" | custom-call | tf_op jit(solution)/shard_map/front/pallas_call | solution.py:557
  39.0 0.0 copy-start.1
  39.0 1.6 %copy-done.1 = bf16[1152,1280]{1,0:T(8,128)(2,1)} copy-done((bf16[1152,1280]{1,0:T(8,128)(2,1)}, bf16[1152,1280]{1,0:T(8,128)(2,1)S(1)}, u32[]{:S(2)}) %copy-start.1) | copy-done | bytes 2949144
  40.6 0.0 copy-start.4
  40.6 0.0 copy-start.7
  40.6 0.0 copy-start.9
  40.6 0.0 copy-start.11
  40.6 0.0 copy-start.13
  40.6 35.5 %tile_steps.1 = (f32[1024,1024]{1,0:T(8,128)}, f32[1024,1024]{1,0:T(8,128)}, bf16[64,64,128]{2,1,0:T(8,128)(2,1)}) custom-call(s32[16,16]{1,0:T(8,128)} %inst_ref.5, s32[16,16]{1,0:T(8,128)} %orient_ref.5, s32[128]{0:T(128)} %owner_ref.5, f32[8]{0:T(128)} %weights_ref.1, bf16[1152,1280]{1,0:T(8,128)(2,1)} %copy-done.1, f32[1024,1024]{1,0:T(8,128)} %target_ref.1, ...), custom_call_target="tpu_custom_call" | custom-call | tf_op jit(solution)/shard_map/tile_steps/pallas_call | solution.py:289
  76.2 0.0 copy-done.4
  76.2 0.0 copy-done.7
  76.2 0.0 copy-start.5
  76.2 1.2 %copy-done.5 = bf16[64,64,128]{2,1,0:T(8,128)(2,1)S(1)} copy-done((bf16[64,64,128]{2,1,0:T(8,128)(2,1)S(1)}, bf16[64,64,128]{2,1,0:T(8,128)(2,1)}, u32[]{:S(2)}) %copy-start.5) | copy-done | bytes 1048600
  77.4 33.7 %update_masters.1 = (bf16[512,64,128]{2,1,0:T(8,128)(2,1)S(1)}, f32[8,64,128]{2,1,0:T(8,128)S(1)}) custom-call(bf16[64,64,128]{2,1,0:T(8,128)(2,1)S(1)} %copy-done.5, f32[8,64,128]{2,1,0:T(8,128)S(1)} %reshape.19.own_ref, bf16[256,256]{1,0:T(8,128)(2,1)S(1)} %copy-done.4, bf16[128,512]{1,0:T(8,128)(2,1)S(1)} %copy-done.7), custom_call_target="tpu_custom_call" | custom-call | tf_op jit(solution)/shard_map/update_masters/pallas_call | solution.py:671
  111.1 0.0 copy-done.9
  111.1 0.0 copy-done.11
  111.1 0.0 copy-done.13
  111.2 0.0 copy-start.2
  111.2 2.2 %copy-done.2 = f32[1024,1024]{1,0:T(8,128)S(1)} copy-done((f32[1024,1024]{1,0:T(8,128)S(1)}, f32[1024,1024]{1,0:T(8,128)}, u32[]{:S(2)}) %copy-start.2) | copy-done | bytes 4194328
  113.3 3.6 %image.1 = f32[1024,1024]{1,0:T(8,128)} custom-call(s32[16,16]{1,0:T(8,128)S(1)} %copy-done.9, s32[16,16]{1,0:T(8,128)S(1)} %copy-done.11, s32[128]{0:T(128)S(1)} %copy-done.13, bf16[512,64,128]{2,1,0:T(8,128)(2,1)S(1)} %get-tuple-element.10.turned_ref, f32[1024,1024]{1,0:T(8,128)S(1)} %copy-done.2), custom_call_target="tpu_custom_call" | custom-call | tf_op jit(solution)/shard_map/image/pallas_call | solution.py:134
  116.9 0.3 reshape.20
  117.3 0.9 reshape.21
  (2 shorter events, 0.1 us)
Async XLA Ops:
  2.5 2.2 %copy-start = (f32[1024,1024]{1,0:T(8,128)S(1)}, f32[1024,1024]{1,0:T(8,128)}, u32[]{:S(2)}) copy-start(f32[1024,1024]{1,0:T(8,128)} %free_ref.3) | copy-start | bytes 12582916
  4.7 0.9 copy-start.3
  5.6 0.9 copy-start.6
  6.5 0.7 copy-start.8
  7.2 0.7 copy-start.10
  7.9 0.7 copy-start.12
  39.0 1.6 %copy-start.1 = (bf16[1152,1280]{1,0:T(8,128)(2,1)}, bf16[1152,1280]{1,0:T(8,128)(2,1)S(1)}, u32[]{:S(2)}) copy-start(bf16[1152,1280]{1,0:T(8,128)(2,1)S(1)} %front.1.padded_ref) | copy-start | bytes 8847364
  40.6 35.6 %copy-start.4 = (bf16[256,256]{1,0:T(8,128)(2,1)S(1)}, bf16[256,256]{1,0:T(8,128)(2,1)}, u32[]{:S(2)}) copy-start(bf16[256,256]{1,0:T(8,128)(2,1)} %constant.34.clone.flip_ref) | copy-start | bytes 393220
  40.6 35.6 %copy-start.7 = (bf16[128,512]{1,0:T(8,128)(2,1)S(1)}, bf16[128,512]{1,0:T(8,128)(2,1)}, u32[]{:S(2)}) copy-start(bf16[128,512]{1,0:T(8,128)(2,1)} %constant.35.clone.spread_ref) | copy-start | bytes 393220
  40.6 70.5 %copy-start.9 = (s32[16,16]{1,0:T(8,128)S(1)}, s32[16,16]{1,0:T(8,128)}, u32[]{:S(2)}) copy-start(s32[16,16]{1,0:T(8,128)} %inst_ref.5) | copy-start | bytes 3076
  40.6 70.5 %copy-start.11 = (s32[16,16]{1,0:T(8,128)S(1)}, s32[16,16]{1,0:T(8,128)}, u32[]{:S(2)}) copy-start(s32[16,16]{1,0:T(8,128)} %orient_ref.5) | copy-start | bytes 3076
  40.6 70.5 %copy-start.13 = (s32[128]{0:T(128)S(1)}, s32[128]{0:T(128)}, u32[]{:S(2)}) copy-start(s32[128]{0:T(128)} %owner_ref.5) | copy-start | bytes 1540
  76.2 1.2 %copy-start.5 = (bf16[64,64,128]{2,1,0:T(8,128)(2,1)S(1)}, bf16[64,64,128]{2,1,0:T(8,128)(2,1)}, u32[]{:S(2)}) copy-start(bf16[64,64,128]{2,1,0:T(8,128)(2,1)} %get-tuple-element.9.sums_ref) | copy-start | bytes 3145732
  111.2 2.2 %copy-start.2 = (f32[1024,1024]{1,0:T(8,128)S(1)}, f32[1024,1024]{1,0:T(8,128)}, u32[]{:S(2)}) copy-start(f32[1024,1024]{1,0:T(8,128)} %get-tuple-element.11.free_ref) | copy-start | bytes 12582916

commit v3 on v2

--- a/solution.py
+++ b/solution.py
@@ -108,16 +108,17 @@
 
 
 def image_kernel(inst_ref, orient_ref, owner_ref, turned_ref, free_ref, out_ref):
-    steps = free_ref.shape[0] // CELL
+    steps = out_ref.shape[0] // CELL
     first = pl.program_id(0) * steps
 
     def step(a, carry):
+        source = pl.ds(pl.multiple_of((first + a) * CELL, CELL), CELL)
         rows = pl.ds(pl.multiple_of(a * CELL, CELL), CELL)
         for pair in range(free_ref.shape[1] // LANES):
             codes = pair_codes(inst_ref, orient_ref, owner_ref, first + a, 2 * pair)
             cells = assemble_pair(turned_ref, codes)
             lanes = slice(pair * LANES, (pair + 1) * LANES)
-            out_ref[rows, lanes] = jnp.tanh(cells + free_ref[rows, lanes])
+            out_ref[rows, lanes] = jnp.tanh(cells + free_ref[source, lanes])
         return carry
 
     lax.fori_loop(0, steps, step, 0)
@@ -136,7 +137,7 @@
         grid_spec=pltpu.PrefetchScalarGridSpec(
             num_scalar_prefetch=3,
             grid=(height // SLAB,),
-            in_specs=[VM, strip],
+            in_specs=[VM, VM],
             out_specs=strip,
         ),
         out_shape=jax.ShapeDtypeStruct(free.shape, jnp.float32),
@@ -146,17 +147,18 @@
 
 
 def tile_kernel(
-    n_row, n_col, inst_ref, orient_ref, owner_ref, weights_ref,
-    padded_ref, target_ref, free_ref, spectra_ref,
+    n_row, n_col, inst_ref, orient_ref, owner_ref,
+    padded_ref, target_ref, free_ref, kern_ref,
     cs_full_ref, cs_lanes_t_ref, cs_g_ref, cs_g_t_ref, field_ref, field_t_ref,
     spread_ref, spread_t_ref, cs_in_ref, cs_in_t_ref, flip_ref,
     resist_ref, new_free_ref, sums_ref,
-    kern_s, half_s, field_s, bhalf_s, level_s, turned_s, sums_s,
+    windows_s, kern_s, half_s, field_s, bhalf_s, level_s, turned_s, left_s, right_s,
+    window_sem, kern_sem,
 ):
     i = pl.program_id(0)
     j = pl.program_id(1)
-    band = spectra_ref.shape[1]
-    kernels = spectra_ref.shape[2]
+    band = kern_s.shape[2]
+    kernels = kern_s.shape[1]
     tile = target_ref.shape[0]
     pad_side = cs_full_ref.shape[1]
     pad_lanes = cs_lanes_t_ref.shape[0]
@@ -164,24 +166,44 @@
     blocks = grid // STRIP
     low = lambda v: v.astype(jnp.bfloat16)
 
-    @pl.when((i == 0) & (j == 0))
+    wide = pl.num_programs(1)
+    step = i * wide + j
+
+    def fetch(n):
+        rows = pl.ds(pl.multiple_of(n // wide * tile, tile), pad_side)
+        lanes = pl.ds(pl.multiple_of(n % wide * tile, tile), pad_lanes)
+        return pltpu.make_async_copy(
+            padded_ref.at[rows, lanes], windows_s.at[n % 2], window_sem.at[n % 2]
+        )
+
+    load_kern = pltpu.make_async_copy(kern_ref, kern_s, kern_sem)
+
+    @pl.when(step == 0)
     def _():
-        sums_s[...] = jnp.zeros_like(sums_s)
-        for k in range(kernels):
-            weight = jnp.full((band, LANES), weights_ref[k], jnp.float32)
-            scale = jnp.sqrt(weight) / (pad_side * band * GAIN_GRID**2)
-            for part in range(2):
-                kern_s[part, k] = spectra_ref[part, :, k, :] * scale
+        fetch(0).start()
+        load_kern.start()
+        left_s[...] = jnp.zeros_like(left_s)
+        right_s[...] = jnp.zeros_like(right_s)
 
     at_row = i * tile
     at_col = j * tile
-    window = padded_ref[
-        pl.ds(pl.multiple_of(at_row, 128), pad_side), pl.ds(pl.multiple_of(at_col, 128), pad_lanes)
-    ]
+    fetch(step).wait()
+
+    @pl.when(step + 1 < pl.num_programs(0) * wide)
+    def _():
+        fetch(step + 1).start()
+
+    here = step % 2
+    window = windows_s[here]
     forw = low(dot(cs_full_ref[...], window))
     spec = dot(forw, cs_lanes_t_ref[...])
     spec_re = spec[:band, :band] + spec[band:, band:]
     spec_im = spec[band:, :band] - spec[:band, band:]
+
+    @pl.when(step == 0)
+    def _():
+        load_kern.wait()
+
     for k in range(kernels):
         amp_re = low(kern_s[0, k] * spec_re - kern_s[1, k] * spec_im)
         amp_im = low(kern_s[0, k] * spec_im + kern_s[1, k] * spec_re)
@@ -200,16 +222,17 @@
     level = level_s[...].reshape(grid, grid)
     mean = jnp.sum(jnp.sum(level, axis=0, keepdims=True), axis=1, keepdims=True) / (grid * grid)
     lines = low(dot(spread_ref[...], low(level - mean)))
-    intensity = dot(lines, spread_t_ref[...]) * (1.0 / GAIN_SPREAD**2) + mean
-    resist = jax.nn.sigmoid(resist_gain * (intensity - resist_level))
+    above = (mean - resist_level) * (0.5 * resist_gain)
+    swing = jnp.tanh(dot(lines, spread_t_ref[...]) * (0.5 * resist_gain / GAIN_SPREAD**2) + above)
+    resist = 0.5 * swing + 0.5
     resist_ref[...] = resist
-    slopes = (4.0 * resist_gain / GAIN_SPREAD**2) * (resist - target_ref[...]) * resist * (1.0 - resist)
+    top = resist_gain / GAIN_SPREAD**2
+    slopes = (resist - target_ref[...]) * (top - top * (swing * swing))
     lines = low(dot(spread_t_ref[...], low(slopes)))
-    level_s[...] = dot(lines, spread_ref[...]).reshape(blocks, STRIP, grid)
+    pulls = low(dot(lines, spread_ref[...])).reshape(blocks, 1, STRIP, grid)
     for b in range(0, blocks, GROUP):
-        pull = level_s[b : b + GROUP].reshape(GROUP, 1, STRIP, grid)
-        pull = jnp.concatenate([pull, pull], axis=3)
-        back = low(field_s[b : b + GROUP].astype(jnp.float32) * pull)
+        pull = jnp.concatenate([pulls[b : b + GROUP]] * 2, axis=3)
+        back = field_s[b : b + GROUP] * pull
         bhalf = low(dot(back.reshape(GROUP * kernels * STRIP, 2 * grid), field_t_ref[...]))
         bhalf = bhalf.reshape(GROUP, kernels, STRIP, grid)
         for g in range(GROUP):
@@ -226,11 +249,11 @@
     lower = jnp.concatenate([low(bspec_im), low(bspec_re)], axis=1)
     bforw = low(dot(jnp.concatenate([upper, lower], axis=0), cs_in_ref[...]))
     gradient = dot(cs_in_t_ref[...], bforw)
-    shading = padded_ref[
-        pl.ds(pl.multiple_of(at_row + HALO, HALO), tile), pl.ds(pl.multiple_of(at_col + LANES, LANES), tile)
-    ].astype(jnp.float32)
+    shading = windows_s[here, HALO : HALO + tile, LANES : LANES + tile].astype(jnp.float32)
     grad_param = gradient * (1.0 - shading * shading)
-    new_free_ref[...] = free_ref[...] - step_free * grad_param
+    new_free_ref[
+        pl.ds(pl.multiple_of(at_row, tile), tile), pl.ds(pl.multiple_of(at_col, tile), tile)
+    ] = free_ref[...] - step_free * grad_param
     turned_s[0] = grad_param
     plain = low(grad_param)
     group = flip_ref.shape[0]
@@ -251,8 +274,8 @@
                 inst_ref, orient_ref, owner_ref, i * cells + a, j * cells + 2 * pair
             )
             lanes = slice(pair * LANES, (pair + 1) * LANES)
-            sums_s[s0] += jnp.where(left, turned_s[o0, rows, lanes], 0.0)
-            sums_s[s1] += jnp.where(left, 0.0, turned_s[o1, rows, lanes])
+            left_s[s0] += turned_s[o0, rows, lanes]
+            right_s[s1] += turned_s[o1, rows, lanes]
         return carry
 
     lax.fori_loop(0, cells, cells_step, 0)
@@ -263,10 +286,8 @@
         share = stored // n_row
 
         def pack(p, carry):
-            one = sums_s[2 * p]
-            two = sums_s[2 * p + 1]
-            one = one + pltpu.roll(one, CELL, 1)
-            two = two + pltpu.roll(two, CELL, 1)
+            one = left_s[2 * p] + pltpu.roll(right_s[2 * p], CELL, 1)
+            two = pltpu.roll(left_s[2 * p + 1], CELL, 1) + right_s[2 * p + 1]
             col = p // stored
             row = p % stored // share
             side = row % 2 * (n_col // 2) + col // 2
@@ -277,30 +298,33 @@
         lax.fori_loop(0, sums_ref.shape[0], pack, 0)
 
 
-def tile_steps(inst, orient, owner, weights, padded, target, free, spectra, consts, flip, masters, n_row, n_col):
+def tile_steps(inst, orient, owner, padded, target, free, kern, consts, flip, masters, n_row, n_col):
     height, width = target.shape
-    band = spectra.shape[1]
-    kernels = spectra.shape[2]
+    kernels, band = kern.shape[1:3]
     grid = 2 * band
     blocks = grid // STRIP
     tile_spec = pl.BlockSpec((TILE, TILE), lambda i, j, *_: (i, j))
+    hbm = pl.BlockSpec(memory_space=pltpu.HBM)
     sums_shape = (masters // 2, CELL, LANES)
-    once = [padded, None, None, spectra, *consts, flip]
     return pl.pallas_call(
         functools.partial(tile_kernel, n_row, n_col),
         grid_spec=pltpu.PrefetchScalarGridSpec(
-            num_scalar_prefetch=4,
+            num_scalar_prefetch=3,
             grid=(height // TILE, width // TILE),
-            in_specs=[tile_spec if v is None else whole_spec(v) for v in once],
-            out_specs=[tile_spec, tile_spec, pl.BlockSpec(sums_shape, lambda *_: (0, 0, 0))],
+            in_specs=[hbm, tile_spec, tile_spec, hbm, *[VM] * len(consts), VM],
+            out_specs=[tile_spec, VM, VM],
             scratch_shapes=[
-                pltpu.VMEM((2, kernels, band, band), jnp.float32),
+                pltpu.VMEM((2, TILE + 2 * HALO, TILE + 2 * LANES), jnp.bfloat16),
+                pltpu.VMEM(kern.shape, jnp.float32),
                 pltpu.VMEM((blocks, kernels, STRIP, grid), jnp.bfloat16),
                 pltpu.VMEM((blocks, kernels, STRIP, 2 * grid), jnp.bfloat16),
                 pltpu.VMEM((kernels, blocks, STRIP, grid), jnp.bfloat16),
                 pltpu.VMEM((blocks, STRIP, grid), jnp.float32),
                 pltpu.VMEM((4, TILE, TILE), jnp.float32),
                 pltpu.VMEM((masters, CELL, LANES), jnp.float32),
+                pltpu.VMEM((masters, CELL, LANES), jnp.float32),
+                pltpu.SemaphoreType.DMA((2,)),
+                pltpu.SemaphoreType.DMA,
             ],
         ),
         out_shape=[
@@ -308,9 +332,9 @@
             jax.ShapeDtypeStruct(target.shape, jnp.float32),
             jax.ShapeDtypeStruct(sums_shape, jnp.bfloat16),
         ],
-        compiler_params=pltpu.CompilerParams(vmem_limit_bytes=60 * 1024 * 1024),
+        compiler_params=pltpu.CompilerParams(vmem_limit_bytes=36 * 1024 * 1024),
         name="tile_steps",
-    )(inst, orient, owner, weights, padded, target, free, spectra, *consts, flip)
+    )(inst, orient, owner, padded, target, free, kern, *consts, flip)
 
 
 def greet(peers):
@@ -347,7 +371,7 @@
     return ids + [(x * 2 + 1 - core, c)]
 
 
-def gather_levels(n_row, n_col, own, table_ref, stored, send_sem, recv_sem, ready):
+def gather_levels(n_row, n_col, own, table_ref, stored, send_sem, recv_sem, started, ready):
     r, c, z, y, x, core, long, z_at, p_at = level_peers(n_row, n_col)
     share = stored // n_row
     partner = (x * 2 + 1 - core, c)
@@ -372,6 +396,7 @@
     first = [make(own, mine, 0, t, (r, z_at(t) * 2 + y)) for t in range(1, long)]
     for copy in first:
         copy.start()
+    started()
     second = []
     third = []
     for t in range(long):
@@ -427,9 +452,10 @@
 
 
 def front_kernel(
-    n_row, n_col, inst_ref, orient_ref, owner_ref, own_ref, free_ref, flip_ref, spread_ref, out_ref,
-    table_s, turned_s, free_s, edge_l, edge_r, from_l, from_r,
-    free_sem, send_sem, recv_sem, halo_send, halo_recv,
+    n_row, n_col, weights_ref, codes_refs, own_ref, free_ref, flip_hbm, spread_hbm, spectra_ref,
+    out_hbm, kern_hbm,
+    out_ref, kern_ref, codes_s, table_s, turned_s, free_s, flip_ref, spread_ref, edge_l, edge_r, from_l, from_r,
+    load_sem, kern_sem, save_sem, send_sem, recv_sem, halo_send, halo_recv,
 ):
     r = lax.axis_index("row")
     c = lax.axis_index("col")
@@ -437,19 +463,41 @@
     packed = height // 2
     stored = own_ref.shape[0]
     share = stored // n_row
-    load_free = pltpu.make_async_copy(free_ref, free_s, free_sem)
-    load_free.start()
+    inst_ref, orient_ref, owner_ref = codes_s
+    band, kernels = kern_ref.shape[2], kern_ref.shape[1]
+    pad_side = TILE + 2 * HALO
+    loads = [(flip_hbm, flip_ref), (spread_hbm, spread_ref), *zip(codes_refs, codes_s), (free_ref, free_s)]
+    loads = [pltpu.make_async_copy(src, dst, load_sem.at[n]) for n, (src, dst) in enumerate(loads)]
+    for part in range(2):
+        for k in range(kernels):
+            src = spectra_ref.at[part, :, k, :]
+            loads.append(pltpu.make_async_copy(src, kern_ref.at[part, k], kern_sem.at[part, k]))
+    for load in loads:
+        load.start()
     moves = [(0, 1), (0, -1), (1, 0), (-1, 0), (1, 1), (1, -1), (-1, 1), (-1, -1)]
     ids = [(lax.rem(r + n_row + dr, n_row), lax.rem(c + n_col + dc, n_col)) for dr, dc in moves]
     greet(gather_ids(n_row, n_col) + ids)
     own = own_ref.at[pl.ds(r * share, share)]
     table_s[pl.ds(c * stored + r * share, share)] = own_ref[pl.ds(r * share, share)]
 
+    def started():
+        for load in loads:
+            load.wait()
+        for k in range(kernels):
+            weight = jnp.full((band, LANES), weights_ref[k], jnp.float32)
+            scale = jnp.sqrt(weight) / (pad_side * band * GAIN_GRID**2)
+            for part in range(2):
+                kern_ref[part, k] = kern_ref[part, k] * scale
+
+    def save(n, *at):
+        return pltpu.make_async_copy(out_ref.at[at], out_hbm.at[at], save_sem.at[n])
+
+    save_kern = pltpu.make_async_copy(kern_ref, kern_hbm, save_sem.at[5])
+
     def ready(at):
         turn_block(table_s, turned_s, flip_ref, spread_ref, at, share)
 
-    gather_levels(n_row, n_col, own, table_s, stored, send_sem, recv_sem, ready)
-    load_free.wait()
+    gather_levels(n_row, n_col, own, table_s, stored, send_sem, recv_sem, started, ready)
 
     pairs = width // LANES
     strips = height // CELL
@@ -522,6 +570,10 @@
     for copy, dst, sends, gets in work:
         pl.when(sends)(copy.start)
     lax.fori_loop(3, strips - 1, inner, 0)
+    lines = slice(HALO, HALO + height)
+    saves = [save(0, lines, middle), save_kern]
+    for copy in saves:
+        copy.start()
     for copy, dst, sends, gets in work:
 
         @pl.when(jnp.logical_not(gets))
@@ -545,38 +597,60 @@
         return carry
 
     lax.fori_loop(0, (height + 2 * HALO) // CELL, unpack, 0)
+    last = [
+        save(1, slice(0, HALO)),
+        save(2, slice(HALO + height, 2 * HALO + height)),
+        save(3, lines, slice(0, LANES)),
+        save(4, lines, slice(LANES + width, 2 * LANES + width)),
+    ]
+    for copy in last:
+        copy.start()
     for copy, dst, sends, gets in work:
         pl.when(sends)(copy.wait_send)
-
-
-def front(inst, orient, owner, own, free, flip, spread, n_row, n_col):
+    for copy in saves + last:
+        copy.wait()
+
+
+def front(codes, weights, own, free, flip, spread, spectra, n_row, n_col):
     height, width = free.shape
     smem = pl.BlockSpec(memory_space=pltpu.SMEM)
+    hbm = pl.BlockSpec(memory_space=pltpu.HBM)
     low = jnp.bfloat16
     pairs = n_col * own.shape[0]
+    band, kernels = spectra.shape[1:3]
     return pl.pallas_call(
         functools.partial(front_kernel, n_row, n_col),
-        in_specs=[smem, smem, smem, VM, pl.BlockSpec(memory_space=pl.ANY), VM, VM],
-        out_specs=VM,
-        out_shape=jax.ShapeDtypeStruct((height + 2 * HALO, width + 2 * LANES), low),
+        in_specs=[smem, [hbm] * 3, VM, hbm, hbm, hbm, hbm],
+        out_specs=[hbm, hbm],
+        out_shape=[
+            jax.ShapeDtypeStruct((height + 2 * HALO, width + 2 * LANES), low),
+            jax.ShapeDtypeStruct((2, kernels, band, band), jnp.float32),
+        ],
         scratch_shapes=[
+            pltpu.VMEM((height + 2 * HALO, width + 2 * LANES), low),
+            pltpu.VMEM((2, kernels, band, band), jnp.float32),
+            [pltpu.SMEM(v.shape, v.dtype) for v in codes],
             pltpu.VMEM((pairs, CELL, LANES), low),
             pltpu.VMEM((8 * pairs, CELL, LANES), low),
             pltpu.VMEM((height, width), jnp.float32),
+            pltpu.VMEM(flip.shape, low),
+            pltpu.VMEM(spread.shape, low),
             pltpu.VMEM((height // 2, LANES), low),
             pltpu.VMEM((height // 2, LANES), low),
             pltpu.VMEM((height // 2 + 2 * HALF, LANES), low),
             pltpu.VMEM((height // 2 + 2 * HALF, LANES), low),
-            pltpu.SemaphoreType.DMA,
+            pltpu.SemaphoreType.DMA((6,)),
+            pltpu.SemaphoreType.DMA((2, kernels)),
+            pltpu.SemaphoreType.DMA((6,)),
             *gather_sems(n_row, n_col),
             pltpu.SemaphoreType.DMA((8,)),
             pltpu.SemaphoreType.DMA((8,)),
         ],
         compiler_params=pltpu.CompilerParams(
-            collective_id=0, has_side_effects=True, vmem_limit_bytes=40 * 1024 * 1024
+            collective_id=0, has_side_effects=True, vmem_limit_bytes=56 * 1024 * 1024
         ),
         name="front",
-    )(inst, orient, owner, own, free, flip, spread)
+    )(weights, codes, own, free, flip, spread, spectra)
 
 
 def smooth_packed(cells):
@@ -655,7 +729,7 @@
     def ready(at):
         turn_block(table_s, turned_ref, flip_ref, spread_ref, at, share)
 
-    gather_levels(n_row, n_col, fresh, table_s, stored, send_sem, recv_sem, ready)
+    gather_levels(n_row, n_col, fresh, table_s, stored, send_sem, recv_sem, lambda: None, ready)
     fresh_ref[...] = high(table_s[pl.ds(c * stored, stored)])
     for copy in [*to_core.values(), *to_p.values(), *to_z.values()]:
         copy.wait_send()
@@ -688,7 +762,7 @@
             *gather_sems(n_row, n_col),
         ],
         compiler_params=pltpu.CompilerParams(
-            collective_id=2, has_side_effects=True, vmem_limit_bytes=32 * 1024 * 1024
+            collective_id=2, has_side_effects=True, vmem_limit_bytes=16 * 1024 * 1024
         ),
         name="update_masters",
     )(sums, own, flip, spread)
@@ -704,13 +778,13 @@
     own = masters.reshape(stored, 2, CELL, CELL).transpose(0, 2, 1, 3).reshape(stored, CELL, LANES)
     n_row = lax.axis_size("row")
     n_col = lax.axis_size("col")
-    padded = front(
-        inst_master, inst_orient, owner_map, own.astype(jnp.bfloat16), tile_free, flip, spread,
+    codes = [inst_master, inst_orient, owner_map]
+    padded, kern = front(
+        codes, socs_weights, own.astype(jnp.bfloat16), tile_free, flip, spread, kernel_spectra,
         n_row, n_col,
     )
     resist, new_free, sums = tile_steps(
-        inst_master, inst_orient, owner_map, socs_weights, padded, target, tile_free,
-        kernel_spectra, consts, flip, total, n_row, n_col,
+        *codes, padded, target, tile_free, kern, consts, flip, total, n_row, n_col
     )
     turned, fresh = update_masters(sums, own, flip, spread, n_row, n_col)
     new_mask = image(inst_master, inst_orient, owner_map, turned, new_free)

time: 119 us -> 111 us (0.933)
  local copies, waits for them, and re-layouts: 14.1 us -> 8.25 us
  Pallas kernels: 103 us -> 101 us
    unnamed x28 -> x36, local copies, waits for them, and re-layouts: 11 us -> 3.15 us
    pallas_call x1, Pallas kernels: 35.5 us -> 31.5 us  [tile_steps(): pl.pallas_call(functools.partial(tile_kernel, n_row, n_col), grid_spec=pl...]
    reshape x3, local copies, waits for them, and re-layouts: 1.85 us -> 3.84 us  [per_device(): masters.reshape(stored, 2, CELL, CELL).transpose(0, 2, 1, 3)]
    pallas_call x1, Pallas kernels: 30.4 us -> 31.7 us  [front(): pl.pallas_call(functools.partial(front_kernel, n_row, n_col), in_specs=[s...]
where the time goes in v3:
time: 111 us
  Pallas kernels  101 us (91%)
  local copies, waits for them, and re-layouts  8.25 us (7%)
    pallas_call x1, Pallas kernels, update_masters(): pl.pallas_call(functools.partial(update_kernel, n_row, n_col), in_specs=[...  34 us
    pallas_call x1, Pallas kernels, front(): pl.pallas_call(functools.partial(front_kernel, n_row, n_col), in_specs=[s...  31.7 us
    pallas_call x1, Pallas kernels, tile_steps(): pl.pallas_call(functools.partial(tile_kernel, n_row, n_col), grid_spec=pl...  31.5 us
    reshape x3, local copies, waits for them, and re-layouts, per_device(): masters.reshape(stored, 2, CELL, CELL).transpose(0, 2, 1, 3)  3.84 us
    pallas_call x1, Pallas kernels, image(): pl.pallas_call(image_kernel, grid_spec=pltpu.PrefetchScalarGridSpec(num_s...  3.59 us
    unnamed x36, local copies, waits for them, and re-layouts  3.15 us

profile of v3, /device:TPU:0, one launch (start us, length us, event | category | flops | bytes accessed | tf_op | source)
XLA Modules:
  0.0 110.7 jit_solution(13047466028486892996)
XLA Ops:
  0.6 0.0 copy-start.2
  0.6 0.0 copy-start.5
  0.7 0.0 copy-start.6
  0.7 0.0 copy-start.7
  0.7 0.0 copy-start.8
  0.7 0.0 copy-start.9
  0.7 0.0 copy-start.10
  0.7 0.0 copy-start.11
  0.7 0.0 copy-start.12
  0.7 0.0 copy-start.13
  0.8 0.0 copy-start.14
  0.8 0.0 copy-start.17
  0.8 0.0 copy-start.16
  0.8 0.0 copy-start.15
  0.8 2.1 %reshape.18 = f32[8,2,64,64]{3,2,1,0:T(8,128)} reshape(f32[16,4096]{1,0:T(8,128)} %param.20) | data formatting | bytes 524288 | tf_op jit(solution)/shard_map/reshape | solution.py:778
  2.9 1.4 %copy.26 = f32[8,2,64,64]{3,1,2,0:T(2,128)S(1)} copy(f32[8,2,64,64]{3,2,1,0:T(8,128)} %reshape.18) | data formatting | bytes 524288 | tf_op jit(solution)/shard_map/reshape | solution.py:778
  4.4 0.3 reshape.19.own_ref
  4.7 0.0 copy-start
  4.7 0.7 convert_element_type.3.own_ref
  5.3 31.7 %front.1 = (bf16[1152,1280]{1,0:T(8,128)(2,1)}, f32[2,8,128,128]{3,2,1,0:T(8,128)}) custom-call(f32[8]{0:T(128)} %weights_ref.1, s32[16,16]{1,0:T(8,128)} %inst_ref.3, s32[16,16]{1,0:T(8,128)} %orient_ref.3, s32[128]{0:T(128)} %owner_ref.3, bf16[8,64,128]{2,1,0:T(8,128)(2,1)} %convert_element_type.3.own_ref, f32[1024,1024]{1,0:T(8,128)} %free_ref.3, ...), custom_call_target="tpu_custom_call" | custom-call | tf_op jit(solution)/shard_map/front/pallas_call | solution.py:621
  37.1 0.0 copy-done.2
  37.1 0.0 copy-done.5
  37.1 0.0 copy-done.6
  37.1 0.0 copy-done.7
  37.1 0.0 copy-done.8
  37.1 0.0 copy-done.9
  37.1 0.0 copy-done.10
  37.1 0.0 copy-done.11
  37.2 0.0 copy-done.12
  37.2 0.0 copy-done.13
  37.2 0.0 copy-done.14
  37.2 0.0 copy-done.17
  37.2 0.0 copy-done.16
  37.2 0.0 copy-done.15
  37.2 0.0 copy-done
  37.2 0.0 copy-start.1
  37.2 1.8 %copy-done.1 = bf16[1152,1280]{1,0:T(8,128)(2,1)S(1)} copy-done((bf16[1152,1280]{1,0:T(8,128)(2,1)S(1)}, bf16[1152,1280]{1,0:T(8,128)(2,1)}, u32[]{:S(2)}) %copy-start.1) | copy-done | bytes 2949144
  39.1 0.0 copy-start.3
  39.1 1.2 %copy-done.3 = f32[2,8,128,128]{3,2,1,0:T(8,128)S(1)} copy-done((f32[2,8,128,128]{3,2,1,0:T(8,128)S(1)}, f32[2,8,128,128]{3,2,1,0:T(8,128)}, u32[]{:S(2)}) %copy-start.3) | copy-done | bytes 1048600
  40.3 0.0 copy-start.4
  40.3 31.5 %tile_steps.1 = (f32[1024,1024]{1,0:T(8,128)}, f32[1024,1024]{1,0:T(8,128)S(1)}, bf16[64,64,128]{2,1,0:T(8,128)(2,1)S(1)}) custom-call(s32[16,16]{1,0:T(8,128)S(1)} %copy-done.15, s32[16,16]{1,0:T(8,128)S(1)} %copy-done.16, s32[128]{0:T(128)S(1)} %copy-done.17, bf16[1152,1280]{1,0:T(8,128)(2,1)S(1)} %copy-done.1, f32[1024,1024]{1,0:T(8,128)S(1)} %copy-done, ...), custom_call_target="tpu_custom_call" | custom-call | tf_op jit(solution)/shard_map/tile_steps/pallas_call | solution.py:309
  71.8 0.0 copy-done.4
  71.8 34.0 %update_masters.1 = (bf16[512,64,128]{2,1,0:T(8,128)(2,1)S(1)}, f32[8,64,128]{2,1,0:T(8,128)S(1)}) custom-call(bf16[64,64,128]{2,1,0:T(8,128)(2,1)S(1)} %get-tuple-element.13.sums_ref, f32[8,64,128]{2,1,0:T(8,128)S(1)} %reshape.19.own_ref, bf16[256,256]{1,0:T(8,128)(2,1)S(1)} %copy-done.2, bf16[128,512]{1,0:T(8,128)(2,1)S(1)} %copy-done.4), custom_call_target="tpu_custom_call" | custom-call | tf_op jit(solution)/shard_map/update_masters/pallas_call | solution.py:745
  105.8 3.6 %image.1 = f32[1024,1024]{1,0:T(8,128)} custom-call(s32[16,16]{1,0:T(8,128)S(1)} %copy-done.15, s32[16,16]{1,0:T(8,128)S(1)} %copy-done.16, s32[128]{0:T(128)S(1)} %copy-done.17, bf16[512,64,128]{2,1,0:T(8,128)(2,1)S(1)} %get-tuple-element.14.turned_ref, f32[1024,1024]{1,0:T(8,128)S(1)} %get-tuple-element.15.free_ref), custom_call_target="tpu_custom_call" | custom-call | tf_op jit(solution)/shard_map/image/pallas_call | solution.py:135
  109.4 0.3 reshape.20
  109.8 0.9 reshape.21
  (1 shorter events, 0.0 us)
Async XLA Ops:
  0.6 36.4 %copy-start.2 = (bf16[256,256]{1,0:T(8,128)(2,1)S(1)}, bf16[256,256]{1,0:T(8,128)(2,1)}, u32[]{:S(2)}) copy-start(bf16[256,256]{1,0:T(8,128)(2,1)} %constant.34.clone.flip_hbm.flip_ref) | copy-start | bytes 393220
  0.6 36.4 %copy-start.5 = (bf16[768,256]{1,0:T(8,128)(2,1)S(1)}, bf16[768,256]{1,0:T(8,128)(2,1)}, u32[]{:S(2)}) copy-start(bf16[768,256]{1,0:T(8,128)(2,1)} %constant.25.clone.cs_lanes_t_ref) | copy-start | bytes 1179652
  0.7 36.4 %copy-start.6 = (bf16[256,640]{1,0:T(8,128)(2,1)S(1)}, bf16[256,640]{1,0:T(8,128)(2,1)}, u32[]{:S(2)}) copy-start(bf16[256,640]{1,0:T(8,128)(2,1)} %constant.24.clone.cs_full_ref) | copy-start | bytes 983044
  0.7 36.4 %copy-start.7 = (bf16[512,256]{1,0:T(8,128)(2,1)S(1)}, bf16[512,256]{1,0:T(8,128)(2,1)}, u32[]{:S(2)}) copy-start(bf16[512,256]{1,0:T(8,128)(2,1)} %constant.33.clone.cs_in_t_ref) | copy-start | bytes 786436
  0.7 36.4 %copy-start.8 = (bf16[256,512]{1,0:T(8,128)(2,1)S(1)}, bf16[256,512]{1,0:T(8,128)(2,1)}, u32[]{:S(2)}) copy-start(bf16[256,512]{1,0:T(8,128)(2,1)} %constant.32.clone.cs_in_ref) | copy-start | bytes 786436
  0.7 36.4 %copy-start.9 = (bf16[256,512]{1,0:T(8,128)(2,1)S(1)}, bf16[256,512]{1,0:T(8,128)(2,1)}, u32[]{:S(2)}) copy-start(bf16[256,512]{1,0:T(8,128)(2,1)} %constant.31.clone.spread_t_ref) | copy-start | bytes 786436
  0.7 36.4 %copy-start.10 = (bf16[512,256]{1,0:T(8,128)(2,1)S(1)}, bf16[512,256]{1,0:T(8,128)(2,1)}, u32[]{:S(2)}) copy-start(bf16[512,256]{1,0:T(8,128)(2,1)} %constant.30.clone.spread_ref) | copy-start | bytes 786436
  0.7 36.4 %copy-start.11 = (bf16[512,256]{1,0:T(8,128)(2,1)S(1)}, bf16[512,256]{1,0:T(8,128)(2,1)}, u32[]{:S(2)}) copy-start(bf16[512,256]{1,0:T(8,128)(2,1)} %constant.29.clone.field_t_ref) | copy-start | bytes 786436
  0.7 36.4 %copy-start.12 = (bf16[256,512]{1,0:T(8,128)(2,1)S(1)}, bf16[256,512]{1,0:T(8,128)(2,1)}, u32[]{:S(2)}) copy-start(bf16[256,512]{1,0:T(8,128)(2,1)} %constant.28.clone.field_ref) | copy-start | bytes 786436
  0.7 36.4 %copy-start.13 = (bf16[256,256]{1,0:T(8,128)(2,1)S(1)}, bf16[256,256]{1,0:T(8,128)(2,1)}, u32[]{:S(2)}) copy-start(bf16[256,256]{1,0:T(8,128)(2,1)} %constant.27.clone.cs_g_t_ref) | copy-start | bytes 393220
  0.8 36.4 %copy-start.14 = (bf16[256,256]{1,0:T(8,128)(2,1)S(1)}, bf16[256,256]{1,0:T(8,128)(2,1)}, u32[]{:S(2)}) copy-start(bf16[256,256]{1,0:T(8,128)(2,1)} %constant.26.clone.cs_g_ref) | copy-start | bytes 393220
  0.8 36.4 %copy-start.17 = (s32[128]{0:T(128)S(1)}, s32[128]{0:T(128)}, u32[]{:S(2)}) copy-start(s32[128]{0:T(128)} %owner_ref.3) | copy-start | bytes 1540
  0.8 36.4 %copy-start.16 = (s32[16,16]{1,0:T(8,128)S(1)}, s32[16,16]{1,0:T(8,128)}, u32[]{:S(2)}) copy-start(s32[16,16]{1,0:T(8,128)} %orient_ref.3) | copy-start | bytes 3076
  0.8 36.4 %copy-start.15 = (s32[16,16]{1,0:T(8,128)S(1)}, s32[16,16]{1,0:T(8,128)}, u32[]{:S(2)}) copy-start(s32[16,16]{1,0:T(8,128)} %inst_ref.3) | copy-start | bytes 3076
  4.7 32.6 %copy-start = (f32[1024,1024]{1,0:T(8,128)S(1)}, f32[1024,1024]{1,0:T(8,128)}, u32[]{:S(2)}) copy-start(f32[1024,1024]{1,0:T(8,128)} %target_ref.1) | copy-start | bytes 12582916
  37.2 1.8 %copy-start.1 = (bf16[1152,1280]{1,0:T(8,128)(2,1)S(1)}, bf16[1152,1280]{1,0:T(8,128)(2,1)}, u32[]{:S(2)}) copy-start(bf16[1152,1280]{1,0:T(8,128)(2,1)} %get-tuple-element.10.padded_ref) | copy-start | bytes 8847364
  39.1 1.2 %copy-start.3 = (f32[2,8,128,128]{3,2,1,0:T(8,128)S(1)}, f32[2,8,128,128]{3,2,1,0:T(8,128)}, u32[]{:S(2)}) copy-start(f32[2,8,128,128]{3,2,1,0:T(8,128)} %get-tuple-element.11.kern_ref) | copy-start | bytes 3145732
  40.3 31.6 %copy-start.4 = (bf16[128,512]{1,0:T(8,128)(2,1)S(1)}, bf16[128,512]{1,0:T(8,128)(2,1)}, u32[]{:S(2)}) copy-start(bf16[128,512]{1,0:T(8,128)(2,1)} %constant.35.clone.spread_hbm.spread_ref) | copy-start | bytes 393220

commit v4 on v3

--- a/solution.py
+++ b/solution.py
@@ -20,6 +20,10 @@
 SLAB = 256
 VM = pl.BlockSpec(memory_space=pltpu.VMEM)
 MESH = pl.DeviceIdType.MESH
+FRONT_MIB = 56
+TILE_MIB = 50
+UPDATE_MIB = 16
+IMAGE_MIB = 8
 GAIN_GRID = 1.9925
 GAIN_SPREAD = 1.725625
 
@@ -84,19 +88,26 @@
     return s0, s1, orient_ref[a, b], orient_ref[a, b + 1]
 
 
-def turn_block(table_ref, turned_ref, flip_ref, spread_ref, at, count):
+def turn_blocks(table_ref, turned_ref, flip_ref, spread_ref, spots, count):
     total = turned_ref.shape[0] // 4
     rows = count * CELL
-    cells = table_ref[pl.ds(at, count)].reshape(rows, LANES)
-    flipped = dot(flip_ref[:rows, :rows], cells).astype(jnp.bfloat16)
-    both = dot(jnp.concatenate([cells, flipped], axis=0), spread_ref[...]).astype(jnp.bfloat16)
-    for f in range(2):
-        for c in range(2):
-            for e in range(2):
-                lanes = slice((2 * c + e) * LANES, (2 * c + e + 1) * LANES)
-                for p in range(count):
-                    start = f * rows + p * CELL
-                    turned_ref[(2 * c + f) * total + 2 * (at + p) + e] = both[start : start + CELL, lanes]
+    most = flip_ref.shape[0] // rows
+    for first in range(0, len(spots), most):
+        some = spots[first : first + most]
+        cells = [table_ref[pl.ds(at, count)].reshape(rows, LANES) for at in some]
+        cells = jnp.concatenate(cells, axis=0) if len(some) > 1 else cells[0]
+        full = len(some) * rows
+        flipped = dot(flip_ref[:full, :full], cells).astype(jnp.bfloat16)
+        both = dot(jnp.concatenate([cells, flipped], axis=0), spread_ref[...]).astype(jnp.bfloat16)
+        for f in range(2):
+            for c in range(2):
+                for e in range(2):
+                    lanes = slice((2 * c + e) * LANES, (2 * c + e + 1) * LANES)
+                    for n, at in enumerate(some):
+                        for p in range(count):
+                            start = f * full + n * rows + p * CELL
+                            spot = (2 * c + f) * total + 2 * (at + p) + e
+                            turned_ref[spot] = both[start : start + CELL, lanes]
 
 
 def assemble_pair(turned_ref, codes):
@@ -112,13 +123,12 @@
     first = pl.program_id(0) * steps
 
     def step(a, carry):
-        source = pl.ds(pl.multiple_of((first + a) * CELL, CELL), CELL)
         rows = pl.ds(pl.multiple_of(a * CELL, CELL), CELL)
         for pair in range(free_ref.shape[1] // LANES):
             codes = pair_codes(inst_ref, orient_ref, owner_ref, first + a, 2 * pair)
             cells = assemble_pair(turned_ref, codes)
             lanes = slice(pair * LANES, (pair + 1) * LANES)
-            out_ref[rows, lanes] = jnp.tanh(cells + free_ref[source, lanes])
+            out_ref[rows, lanes] = jnp.tanh(cells + free_ref[rows, lanes])
         return carry
 
     lax.fori_loop(0, steps, step, 0)
@@ -137,18 +147,19 @@
         grid_spec=pltpu.PrefetchScalarGridSpec(
             num_scalar_prefetch=3,
             grid=(height // SLAB,),
-            in_specs=[VM, VM],
+            in_specs=[VM, strip],
             out_specs=strip,
         ),
         out_shape=jax.ShapeDtypeStruct(free.shape, jnp.float32),
-        compiler_params=pltpu.CompilerParams(vmem_limit_bytes=8 * 1024 * 1024),
+        compiler_params=pltpu.CompilerParams(vmem_limit_bytes=IMAGE_MIB * 1024 * 1024),
+        input_output_aliases={4: 0},
         name="image",
     )(inst, orient, owner, turned, free)
 
 
 def tile_kernel(
-    n_row, n_col, inst_ref, orient_ref, owner_ref,
-    padded_ref, target_ref, free_ref, kern_ref,
+    n_row, n_col, inst_ref, orient_ref, owner_ref, weights_ref,
+    padded_ref, target_ref, free_ref, spectra_ref,
     cs_full_ref, cs_lanes_t_ref, cs_g_ref, cs_g_t_ref, field_ref, field_t_ref,
     spread_ref, spread_t_ref, cs_in_ref, cs_in_t_ref, flip_ref,
     resist_ref, new_free_ref, sums_ref,
@@ -176,17 +187,20 @@
             padded_ref.at[rows, lanes], windows_s.at[n % 2], window_sem.at[n % 2]
         )
 
-    load_kern = pltpu.make_async_copy(kern_ref, kern_s, kern_sem)
+    def load_kern(part, k):
+        return pltpu.make_async_copy(
+            spectra_ref.at[part, :, k, :], kern_s.at[part, k], kern_sem.at[part, k]
+        )
 
     @pl.when(step == 0)
     def _():
         fetch(0).start()
-        load_kern.start()
+        for k in range(kernels):
+            load_kern(0, k).start()
+            load_kern(1, k).start()
         left_s[...] = jnp.zeros_like(left_s)
         right_s[...] = jnp.zeros_like(right_s)
 
-    at_row = i * tile
-    at_col = j * tile
     fetch(step).wait()
 
     @pl.when(step + 1 < pl.num_programs(0) * wide)
@@ -202,7 +216,12 @@
 
     @pl.when(step == 0)
     def _():
-        load_kern.wait()
+        for k in range(kernels):
+            weight = jnp.full((band, LANES), weights_ref[k], jnp.float32)
+            scale = jnp.sqrt(weight) / (pad_side * band * GAIN_GRID**2)
+            for part in range(2):
+                load_kern(part, k).wait()
+                kern_s[part, k] = kern_s[part, k] * scale
 
     for k in range(kernels):
         amp_re = low(kern_s[0, k] * spec_re - kern_s[1, k] * spec_im)
@@ -251,9 +270,7 @@
     gradient = dot(cs_in_t_ref[...], bforw)
     shading = windows_s[here, HALO : HALO + tile, LANES : LANES + tile].astype(jnp.float32)
     grad_param = gradient * (1.0 - shading * shading)
-    new_free_ref[
-        pl.ds(pl.multiple_of(at_row, tile), tile), pl.ds(pl.multiple_of(at_col, tile), tile)
-    ] = free_ref[...] - step_free * grad_param
+    new_free_ref[...] = free_ref[...] - step_free * grad_param
     turned_s[0] = grad_param
     plain = low(grad_param)
     group = flip_ref.shape[0]
@@ -295,12 +312,14 @@
             sums_ref[spot] = low(jnp.where(left, one, two))
             return carry
 
-        lax.fori_loop(0, sums_ref.shape[0], pack, 0)
-
-
-def tile_steps(inst, orient, owner, padded, target, free, kern, consts, flip, masters, n_row, n_col):
+        lax.fori_loop(0, sums_ref.shape[0], pack, 0, unroll=4)
+
+
+def tile_steps(
+    inst, orient, owner, weights, padded, target, free, spectra, consts, flip, masters, n_row, n_col
+):
     height, width = target.shape
-    kernels, band = kern.shape[1:3]
+    band, kernels = spectra.shape[1:3]
     grid = 2 * band
     blocks = grid // STRIP
     tile_spec = pl.BlockSpec((TILE, TILE), lambda i, j, *_: (i, j))
@@ -309,13 +328,13 @@
     return pl.pallas_call(
         functools.partial(tile_kernel, n_row, n_col),
         grid_spec=pltpu.PrefetchScalarGridSpec(
-            num_scalar_prefetch=3,
+            num_scalar_prefetch=4,
             grid=(height // TILE, width // TILE),
             in_specs=[hbm, tile_spec, tile_spec, hbm, *[VM] * len(consts), VM],
-            out_specs=[tile_spec, VM, VM],
+            out_specs=[tile_spec, tile_spec, VM],
             scratch_shapes=[
                 pltpu.VMEM((2, TILE + 2 * HALO, TILE + 2 * LANES), jnp.bfloat16),
-                pltpu.VMEM(kern.shape, jnp.float32),
+                pltpu.VMEM((2, kernels, band, band), jnp.float32),
                 pltpu.VMEM((blocks, kernels, STRIP, grid), jnp.bfloat16),
                 pltpu.VMEM((blocks, kernels, STRIP, 2 * grid), jnp.bfloat16),
                 pltpu.VMEM((kernels, blocks, STRIP, grid), jnp.bfloat16),
@@ -324,7 +343,7 @@
                 pltpu.VMEM((masters, CELL, LANES), jnp.float32),
                 pltpu.VMEM((masters, CELL, LANES), jnp.float32),
                 pltpu.SemaphoreType.DMA((2,)),
-                pltpu.SemaphoreType.DMA,
+                pltpu.SemaphoreType.DMA((2, kernels)),
             ],
         ),
         out_shape=[
@@ -332,9 +351,9 @@
             jax.ShapeDtypeStruct(target.shape, jnp.float32),
             jax.ShapeDtypeStruct(sums_shape, jnp.bfloat16),
         ],
-        compiler_params=pltpu.CompilerParams(vmem_limit_bytes=36 * 1024 * 1024),
+        compiler_params=pltpu.CompilerParams(vmem_limit_bytes=TILE_MIB * 1024 * 1024),
         name="tile_steps",
-    )(inst, orient, owner, padded, target, free, kern, *consts, flip)
+    )(inst, orient, owner, weights, padded, target, free, spectra, *consts, flip)
 
 
 def greet(peers):
@@ -412,35 +431,48 @@
         copy = make(src, at, 2, t * n_row, partner)
         copy.start()
         third.append(copy)
-    for t in range(long):
-        ready(first_row(r, z_at(-t) * 2 + y))
-
-    def across(n, carry):
+    ready([first_row(r, z_at(-t) * 2 + y) for t in range(long)])
+
+    def across(n):
         t = n // (n_row - 1)
         q = n % (n_row - 1) + 1
-        slot = t * n_row + q
         px, py = p_at(-q)
         at = first_row(px * 2 + core, z_at(-t) * 2 + py)
+        slot = t * n_row + q
         make(here(at), at, 1, slot, partner).wait_recv()
         make(here(at), at, 2, slot, partner).start()
-        ready(at)
-        return carry
-
-    def beside(n, carry):
-        t = n // n_row
-        q = n % n_row
+        return at
+
+    def beside(t, q):
         px, py = p_at(-q)
         at = first_row(px * 2 + 1 - core, z_at(-t) * 2 + py)
-        make(here(at), at, 2, n, partner).wait_recv()
-        ready(at)
-        return carry
+        make(here(at), at, 2, t * n_row + q, partner).wait_recv()
+        return at
+
+    def later(n):
+        return beside(n // (n_row - 1), n % (n_row - 1) + 1)
+
+    def early(n, carry):
+        ready([across(n), beside(n, 0)])
+        return carry
+
+    def middle(n, carry):
+        ready([across(n), later(n - long)])
+        return carry
+
+    def late(n, carry):
+        ready([later(2 * n), later(2 * n + 1)])
+        return carry
+
+    count = long * (n_row - 1)
+    lax.fori_loop(0, long, early, 0)
+    lax.fori_loop(long, count, middle, 0)
+    lax.fori_loop((count - long) // 2, count // 2, late, 0)
 
     def sent(n, carry):
         make(here(mine), mine, 2, n, partner).wait_send()
         return carry
 
-    lax.fori_loop(0, long * (n_row - 1), across, 0)
-    lax.fori_loop(0, long * n_row, beside, 0)
     for copy in first + second:
         copy.wait_send()
     lax.fori_loop(0, long * n_row, sent, 0)
@@ -451,53 +483,62 @@
     return [pltpu.SemaphoreType.DMA(shape), pltpu.SemaphoreType.DMA(shape)]
 
 
+def pack_rows(rows_ref, lines_s, out_ref):
+    left = left_mask(HALF)
+    for pair in range(out_ref.shape[0]):
+        halves = []
+        for e in range(2):
+            for n in range(HALF):
+                at = 2 * pair + e
+                lines_s[at, n : n + 1] = rows_ref[at : at + 1, n * LANES : (n + 1) * LANES]
+            halves.append(lines_s[2 * pair + e])
+        one, two = halves
+        even = jnp.where(left, one, pltpu.roll(two, CELL, 1))
+        odd = jnp.where(left, pltpu.roll(one, CELL, 1), two)
+        out_ref[pair, pl.ds(0, HALF, stride=2)] = even
+        out_ref[pair, pl.ds(1, HALF, stride=2)] = odd
+
+
 def front_kernel(
-    n_row, n_col, weights_ref, codes_refs, own_ref, free_ref, flip_hbm, spread_hbm, spectra_ref,
-    out_hbm, kern_hbm,
-    out_ref, kern_ref, codes_s, table_s, turned_s, free_s, flip_ref, spread_ref, edge_l, edge_r, from_l, from_r,
-    load_sem, kern_sem, save_sem, send_sem, recv_sem, halo_send, halo_recv,
+    n_row, n_col, codes_refs, rows_hbm, free_ref, flip_hbm, spread_hbm, out_hbm, own_ref,
+    out_ref, codes_s, rows_s, lines_s, cells_s, share_s, table_s, turned_s, free_s, flip_ref, spread_ref,
+    edge_l, edge_r, from_l, from_r,
+    load_sem, save_sem, send_sem, recv_sem, halo_send, halo_recv,
 ):
     r = lax.axis_index("row")
     c = lax.axis_index("col")
     height, width = free_s.shape
     packed = height // 2
-    stored = own_ref.shape[0]
+    stored = rows_s.shape[0] // 2
     share = stored // n_row
     inst_ref, orient_ref, owner_ref = codes_s
-    band, kernels = kern_ref.shape[2], kern_ref.shape[1]
-    pad_side = TILE + 2 * HALO
-    loads = [(flip_hbm, flip_ref), (spread_hbm, spread_ref), *zip(codes_refs, codes_s), (free_ref, free_s)]
+    loads = [(rows_hbm, rows_s), (flip_hbm, flip_ref), (spread_hbm, spread_ref)]
+    loads += [*zip(codes_refs, codes_s), (free_ref, free_s)]
     loads = [pltpu.make_async_copy(src, dst, load_sem.at[n]) for n, (src, dst) in enumerate(loads)]
-    for part in range(2):
-        for k in range(kernels):
-            src = spectra_ref.at[part, :, k, :]
-            loads.append(pltpu.make_async_copy(src, kern_ref.at[part, k], kern_sem.at[part, k]))
     for load in loads:
         load.start()
+    loads[0].wait()
+    pack_rows(rows_s, lines_s, cells_s)
+    own_ref[...] = cells_s[pl.ds(r * share, share)]
+    share_s[...] = own_ref[...].astype(jnp.bfloat16)
     moves = [(0, 1), (0, -1), (1, 0), (-1, 0), (1, 1), (1, -1), (-1, 1), (-1, -1)]
     ids = [(lax.rem(r + n_row + dr, n_row), lax.rem(c + n_col + dc, n_col)) for dr, dc in moves]
     greet(gather_ids(n_row, n_col) + ids)
-    own = own_ref.at[pl.ds(r * share, share)]
-    table_s[pl.ds(c * stored + r * share, share)] = own_ref[pl.ds(r * share, share)]
+    table_s[pl.ds(c * stored + r * share, share)] = share_s[...]
 
     def started():
-        for load in loads:
-            load.wait()
-        for k in range(kernels):
-            weight = jnp.full((band, LANES), weights_ref[k], jnp.float32)
-            scale = jnp.sqrt(weight) / (pad_side * band * GAIN_GRID**2)
-            for part in range(2):
-                kern_ref[part, k] = kern_ref[part, k] * scale
+        loads[1].wait()
+        loads[2].wait()
 
     def save(n, *at):
         return pltpu.make_async_copy(out_ref.at[at], out_hbm.at[at], save_sem.at[n])
 
-    save_kern = pltpu.make_async_copy(kern_ref, kern_hbm, save_sem.at[5])
-
-    def ready(at):
-        turn_block(table_s, turned_s, flip_ref, spread_ref, at, share)
-
-    gather_levels(n_row, n_col, own, table_s, stored, send_sem, recv_sem, started, ready)
+    def ready(spots):
+        turn_blocks(table_s, turned_s, flip_ref, spread_ref, spots, share)
+
+    gather_levels(n_row, n_col, share_s, table_s, stored, send_sem, recv_sem, started, ready)
+    for load in loads[3:]:
+        load.wait()
 
     pairs = width // LANES
     strips = height // CELL
@@ -571,7 +612,7 @@
         pl.when(sends)(copy.start)
     lax.fori_loop(3, strips - 1, inner, 0)
     lines = slice(HALO, HALO + height)
-    saves = [save(0, lines, middle), save_kern]
+    saves = [save(0, lines, middle)]
     for copy in saves:
         copy.start()
     for copy, dst, sends, gets in work:
@@ -611,46 +652,47 @@
         copy.wait()
 
 
-def front(codes, weights, own, free, flip, spread, spectra, n_row, n_col):
+def front(codes, masters, free, flip, spread, n_row, n_col):
     height, width = free.shape
-    smem = pl.BlockSpec(memory_space=pltpu.SMEM)
     hbm = pl.BlockSpec(memory_space=pltpu.HBM)
     low = jnp.bfloat16
-    pairs = n_col * own.shape[0]
-    band, kernels = spectra.shape[1:3]
+    stored = masters.shape[0] // 2
+    pairs = n_col * stored
+    cells = (CELL, LANES)
+    edge = pltpu.VMEM((height // 2, LANES), low)
+    edge_in = pltpu.VMEM((height // 2 + 2 * HALF, LANES), low)
     return pl.pallas_call(
         functools.partial(front_kernel, n_row, n_col),
-        in_specs=[smem, [hbm] * 3, VM, hbm, hbm, hbm, hbm],
-        out_specs=[hbm, hbm],
+        in_specs=[[hbm] * 3, hbm, hbm, hbm, hbm],
+        out_specs=[hbm, VM],
         out_shape=[
             jax.ShapeDtypeStruct((height + 2 * HALO, width + 2 * LANES), low),
-            jax.ShapeDtypeStruct((2, kernels, band, band), jnp.float32),
+            jax.ShapeDtypeStruct((stored // n_row,) + cells, jnp.float32),
         ],
         scratch_shapes=[
             pltpu.VMEM((height + 2 * HALO, width + 2 * LANES), low),
-            pltpu.VMEM((2, kernels, band, band), jnp.float32),
             [pltpu.SMEM(v.shape, v.dtype) for v in codes],
-            pltpu.VMEM((pairs, CELL, LANES), low),
-            pltpu.VMEM((8 * pairs, CELL, LANES), low),
+            pltpu.VMEM(masters.shape, jnp.float32),
+            pltpu.VMEM((2 * stored, HALF, LANES), jnp.float32),
+            pltpu.VMEM((stored,) + cells, jnp.float32),
+            pltpu.VMEM((stored // n_row,) + cells, low),
+            pltpu.VMEM((pairs,) + cells, low),
+            pltpu.VMEM((8 * pairs,) + cells, low),
             pltpu.VMEM((height, width), jnp.float32),
             pltpu.VMEM(flip.shape, low),
             pltpu.VMEM(spread.shape, low),
-            pltpu.VMEM((height // 2, LANES), low),
-            pltpu.VMEM((height // 2, LANES), low),
-            pltpu.VMEM((height // 2 + 2 * HALF, LANES), low),
-            pltpu.VMEM((height // 2 + 2 * HALF, LANES), low),
-            pltpu.SemaphoreType.DMA((6,)),
-            pltpu.SemaphoreType.DMA((2, kernels)),
-            pltpu.SemaphoreType.DMA((6,)),
+            edge, edge, edge_in, edge_in,
+            pltpu.SemaphoreType.DMA((7,)),
+            pltpu.SemaphoreType.DMA((5,)),
             *gather_sems(n_row, n_col),
             pltpu.SemaphoreType.DMA((8,)),
             pltpu.SemaphoreType.DMA((8,)),
         ],
         compiler_params=pltpu.CompilerParams(
-            collective_id=0, has_side_effects=True, vmem_limit_bytes=56 * 1024 * 1024
+            collective_id=0, has_side_effects=True, vmem_limit_bytes=FRONT_MIB * 1024 * 1024
         ),
         name="front",
-    )(weights, codes, own, free, flip, spread, spectra)
+    )(codes, masters, free, flip, spread)
 
 
 def smooth_packed(cells):
@@ -672,8 +714,8 @@
 ):
     r, c, z, y, x, core, long, z_at, p_at = level_peers(n_row, n_col)
     p = x * 2 + y
-    stored = own_ref.shape[0]
-    share = stored // n_row
+    share = own_ref.shape[0]
+    stored = share * n_row
     low = lambda v: v.astype(jnp.bfloat16)
     high = lambda v: v.astype(jnp.float32)
     greet(gather_ids(n_row, n_col))
@@ -721,13 +763,13 @@
     for t in range(1, long):
         to_z[t].wait_recv()
         total = total + high(rz[t])
-    updated = own_ref[pl.ds(r * share, share)] - step_master * total
+    updated = own_ref[...] - step_master * total
     value = low(smooth_packed(updated))
     fresh[...] = value
     table_s[pl.ds(c * stored + r * share, share)] = value
 
-    def ready(at):
-        turn_block(table_s, turned_ref, flip_ref, spread_ref, at, share)
+    def ready(spots):
+        turn_blocks(table_s, turned_ref, flip_ref, spread_ref, spots, share)
 
     gather_levels(n_row, n_col, fresh, table_s, stored, send_sem, recv_sem, lambda: None, ready)
     fresh_ref[...] = high(table_s[pl.ds(c * stored, stored)])
@@ -736,9 +778,9 @@
 
 
 def update_masters(sums, own, flip, spread, n_row, n_col):
-    stored = own.shape[0]
+    share = own.shape[0]
+    stored = share * n_row
     long = n_col // 2
-    share = stored // n_row
     low = jnp.bfloat16
     cells = (CELL, LANES)
     sems = [pltpu.SemaphoreType.DMA((n,)) for n in (long, long, long * n_row, long * n_row, long, long)]
@@ -748,7 +790,7 @@
         out_specs=[VM, VM],
         out_shape=[
             jax.ShapeDtypeStruct((8 * sums.shape[0],) + cells, low),
-            jax.ShapeDtypeStruct(own.shape, jnp.float32),
+            jax.ShapeDtypeStruct((stored,) + cells, jnp.float32),
         ],
         scratch_shapes=[
             pltpu.VMEM(sums.shape, low),
@@ -762,7 +804,7 @@
             *gather_sems(n_row, n_col),
         ],
         compiler_params=pltpu.CompilerParams(
-            collective_id=2, has_side_effects=True, vmem_limit_bytes=16 * 1024 * 1024
+            collective_id=2, has_side_effects=True, vmem_limit_bytes=UPDATE_MIB * 1024 * 1024
         ),
         name="update_masters",
     )(sums, own, flip, spread)
@@ -775,16 +817,13 @@
     total = owner_map.shape[0]
     consts = tables(TILE + 2 * HALO, kernel_spectra.shape[1], HALO, TILE)
     flip, spread = flips()
-    own = masters.reshape(stored, 2, CELL, CELL).transpose(0, 2, 1, 3).reshape(stored, CELL, LANES)
     n_row = lax.axis_size("row")
     n_col = lax.axis_size("col")
     codes = [inst_master, inst_orient, owner_map]
-    padded, kern = front(
-        codes, socs_weights, own.astype(jnp.bfloat16), tile_free, flip, spread, kernel_spectra,
+    padded, own = front(codes, masters, tile_free, flip, spread, n_row, n_col)
+    resist, new_free, sums = tile_steps(
+        *codes, socs_weights, padded, target, tile_free, kernel_spectra, consts, flip, total,
         n_row, n_col,
-    )
-    resist, new_free, sums = tile_steps(
-        *codes, padded, target, tile_free, kern, consts, flip, total, n_row, n_col
     )
     turned, fresh = update_masters(sums, own, flip, spread, n_row, n_col)
     new_mask = image(inst_master, inst_orient, owner_map, turned, new_free)

time: 111 us -> 97.6 us (0.88)
  local copies, waits for them, and re-layouts: 8.25 us -> 1.36 us
  Pallas kernels: 101 us -> 95 us
    pallas_call x1, Pallas kernels: 34 us -> 29.6 us  [update_masters(): pl.pallas_call(functools.partial(update_kernel, n_row, n_col), in_specs=[...]
    reshape x3 -> x0, local copies, waits for them, and re-layouts: 3.84 us -> none  [per_device(): masters.reshape(stored, 2, CELL, CELL).transpose(0, 2, 1, 3)]
    unnamed x36 -> x34, local copies, waits for them, and re-layouts: 3.15 us -> 0.1 us
    pallas_call x1, Pallas kernels: 3.59 us -> 5.84 us  [image(): pl.pallas_call(image_kernel, grid_spec=pltpu.PrefetchScalarGridSpec(num_s...]
    pallas_call x1, Pallas kernels: 31.7 us -> 29.8 us  [front(): pl.pallas_call(functools.partial(front_kernel, n_row, n_col), in_specs=[[...]
    pallas_call x1, Pallas kernels: 31.5 us -> 29.7 us  [tile_steps(): pl.pallas_call(functools.partial(tile_kernel, n_row, n_col), grid_spec=pl...]
where the time goes in v4:
time: 97.6 us; the launch traced here: 97.3 us
  Pallas kernels  95 us (97%)
  local copies, waits for them, and re-layouts  1.36 us (1%)
    pallas_call x1, Pallas kernels, front(): pl.pallas_call(functools.partial(front_kernel, n_row, n_col), in_specs=[[...  29.8 us
    pallas_call x1, Pallas kernels, tile_steps(): pl.pallas_call(functools.partial(tile_kernel, n_row, n_col), grid_spec=pl...  29.7 us
    pallas_call x1, Pallas kernels, update_masters(): pl.pallas_call(functools.partial(update_kernel, n_row, n_col), in_specs=[...  29.6 us
    pallas_call x1, Pallas kernels, image(): pl.pallas_call(image_kernel, grid_spec=pltpu.PrefetchScalarGridSpec(num_s...  5.84 us

profile of v4, /device:TPU:0, one launch (start us, length us, event | category | flops | bytes accessed | tf_op | source)
XLA Modules:
  0.0 97.3 jit_solution(15158722564150457264)
XLA Ops:
  0.6 0.0 copy-start
  0.6 0.0 copy-start.4
  0.7 0.0 copy-start.5
  0.7 0.0 copy-start.6
  0.7 0.0 copy-start.7
  0.7 0.0 copy-start.8
  0.7 0.0 copy-start.9
  0.7 0.0 copy-start.10
  0.7 0.0 copy-start.11
  0.7 0.0 copy-start.2
  0.8 0.0 copy-start.3
  0.8 0.0 copy-start.15
  0.8 0.0 copy-start.13
  0.8 0.0 copy-start.12
  0.8 0.0 copy-start.16
  0.8 29.8 %front.1 = (bf16[1152,1280]{1,0:T(8,128)(2,1)}, f32[2,64,128]{2,1,0:T(8,128)}) custom-call(s32[16,16]{1,0:T(8,128)} %inst_ref.3, s32[16,16]{1,0:T(8,128)} %orient_ref.3, s32[128]{0:T(128)} %owner_ref.3, f32[16,4096]{1,0:T(8,128)} %rows_hbm.1, f32[1024,1024]{1,0:T(8,128)} %free_ref.3, bf16[256,256]{1,0:T(8,128)(2,1)} %constant.34.clone.flip_hbm.flip_ref, ...), custom_call_target="tpu_custom_call" | custom-call | tf_op jit(solution)/shard_map/front/pallas_call | solution.py:664
  30.7 0.0 copy-done
  30.7 0.0 copy-done.4
  30.7 0.0 copy-done.5
  30.7 0.0 copy-done.6
  30.7 0.0 copy-done.7
  30.7 0.0 copy-done.8
  30.7 0.0 copy-done.9
  30.7 0.0 copy-done.10
  30.7 0.0 copy-done.11
  30.7 0.0 copy-done.2
  30.8 0.0 copy-done.3
  30.8 0.0 copy-done.15
  30.8 0.0 copy-done.13
  30.8 0.0 copy-done.12
  30.8 0.0 copy-done.16
  30.8 0.0 copy-start.1
  30.8 0.0 copy-start.14
  30.8 29.7 %tile_steps.1 = (f32[1024,1024]{1,0:T(8,128)}, f32[1024,1024]{1,0:T(8,128)}, bf16[64,64,128]{2,1,0:T(8,128)(2,1)S(1)}) custom-call(s32[16,16]{1,0:T(8,128)S(1)} %copy-done.12, s32[16,16]{1,0:T(8,128)S(1)} %copy-done.13, s32[128]{0:T(128)S(1)} %copy-done.15, f32[8]{0:T(128)S(1)} %copy-done.16, bf16[1152,1280]{1,0:T(8,128)(2,1)} %get-tuple-element.10.padded_ref, ...), custom_call_target="tpu_custom_call" | custom-call | tf_op jit(solution)/shard_map/tile_steps/pallas_call | solution.py:328
  60.6 0.0 copy-done.1
  60.6 0.0 copy-done.14
  60.6 29.6 %update_masters.1 = (bf16[512,64,128]{2,1,0:T(8,128)(2,1)S(1)}, f32[8,64,128]{2,1,0:T(8,128)S(1)}) custom-call(bf16[64,64,128]{2,1,0:T(8,128)(2,1)S(1)} %get-tuple-element.12.sums_ref, f32[2,64,128]{2,1,0:T(8,128)S(1)} %copy-done.14, bf16[256,256]{1,0:T(8,128)(2,1)S(1)} %copy-done, bf16[128,512]{1,0:T(8,128)(2,1)S(1)} %copy-done.1), custom_call_target="tpu_custom_call" | custom-call | tf_op jit(solution)/shard_map/update_masters/pallas_call | solution.py:787
  90.2 5.8 %image.1 = f32[1024,1024]{1,0:T(8,128)} custom-call(s32[16,16]{1,0:T(8,128)S(1)} %copy-done.12, s32[16,16]{1,0:T(8,128)S(1)} %copy-done.13, s32[128]{0:T(128)S(1)} %copy-done.15, bf16[512,64,128]{2,1,0:T(8,128)(2,1)S(1)} %get-tuple-element.14.turned_ref, f32[1024,1024]{1,0:T(8,128)} %get-tuple-element.15.free_ref), custom_call_target="tpu_custom_call", output_to_operand_aliasing={{}: (4, {})} | custom-call | tf_op jit(solution)/shard_map/image/pallas_call | solution.py:145
  96.1 0.3 reshape.12
  96.4 0.9 reshape.13
  (1 shorter events, 0.0 us)
Async XLA Ops:
  0.6 30.0 %copy-start = (bf16[256,256]{1,0:T(8,128)(2,1)S(1)}, bf16[256,256]{1,0:T(8,128)(2,1)}, u32[]{:S(2)}) copy-start(bf16[256,256]{1,0:T(8,128)(2,1)} %constant.34.clone.flip_hbm.flip_ref) | copy-start | bytes 393220
  0.6 30.0 %copy-start.4 = (bf16[512,256]{1,0:T(8,128)(2,1)S(1)}, bf16[512,256]{1,0:T(8,128)(2,1)}, u32[]{:S(2)}) copy-start(bf16[512,256]{1,0:T(8,128)(2,1)} %constant.33.clone.cs_in_t_ref) | copy-start | bytes 786436
  0.7 30.0 %copy-start.5 = (bf16[256,512]{1,0:T(8,128)(2,1)S(1)}, bf16[256,512]{1,0:T(8,128)(2,1)}, u32[]{:S(2)}) copy-start(bf16[256,512]{1,0:T(8,128)(2,1)} %constant.32.clone.cs_in_ref) | copy-start | bytes 786436
  0.7 30.0 %copy-start.6 = (bf16[256,512]{1,0:T(8,128)(2,1)S(1)}, bf16[256,512]{1,0:T(8,128)(2,1)}, u32[]{:S(2)}) copy-start(bf16[256,512]{1,0:T(8,128)(2,1)} %constant.31.clone.spread_t_ref) | copy-start | bytes 786436
  0.7 30.0 %copy-start.7 = (bf16[512,256]{1,0:T(8,128)(2,1)S(1)}, bf16[512,256]{1,0:T(8,128)(2,1)}, u32[]{:S(2)}) copy-start(bf16[512,256]{1,0:T(8,128)(2,1)} %constant.30.clone.spread_ref) | copy-start | bytes 786436
  0.7 30.0 %copy-start.8 = (bf16[512,256]{1,0:T(8,128)(2,1)S(1)}, bf16[512,256]{1,0:T(8,128)(2,1)}, u32[]{:S(2)}) copy-start(bf16[512,256]{1,0:T(8,128)(2,1)} %constant.29.clone.field_t_ref) | copy-start | bytes 786436
  0.7 30.0 %copy-start.9 = (bf16[256,512]{1,0:T(8,128)(2,1)S(1)}, bf16[256,512]{1,0:T(8,128)(2,1)}, u32[]{:S(2)}) copy-start(bf16[256,512]{1,0:T(8,128)(2,1)} %constant.28.clone.field_ref) | copy-start | bytes 786436
  0.7 30.0 %copy-start.10 = (bf16[256,256]{1,0:T(8,128)(2,1)S(1)}, bf16[256,256]{1,0:T(8,128)(2,1)}, u32[]{:S(2)}) copy-start(bf16[256,256]{1,0:T(8,128)(2,1)} %constant.27.clone.cs_g_t_ref) | copy-start | bytes 393220
  0.7 30.0 %copy-start.11 = (bf16[256,256]{1,0:T(8,128)(2,1)S(1)}, bf16[256,256]{1,0:T(8,128)(2,1)}, u32[]{:S(2)}) copy-start(bf16[256,256]{1,0:T(8,128)(2,1)} %constant.26.clone.cs_g_ref) | copy-start | bytes 393220
  0.7 30.0 %copy-start.2 = (bf16[768,256]{1,0:T(8,128)(2,1)S(1)}, bf16[768,256]{1,0:T(8,128)(2,1)}, u32[]{:S(2)}) copy-start(bf16[768,256]{1,0:T(8,128)(2,1)} %constant.25.clone.cs_lanes_t_ref) | copy-start | bytes 1179652
  0.8 30.0 %copy-start.3 = (bf16[256,640]{1,0:T(8,128)(2,1)S(1)}, bf16[256,640]{1,0:T(8,128)(2,1)}, u32[]{:S(2)}) copy-start(bf16[256,640]{1,0:T(8,128)(2,1)} %constant.24.clone.cs_full_ref) | copy-start | bytes 983044
  0.8 30.0 %copy-start.15 = (s32[128]{0:T(128)S(1)}, s32[128]{0:T(128)}, u32[]{:S(2)}) copy-start(s32[128]{0:T(128)} %owner_ref.3) | copy-start | bytes 1540
  0.8 30.0 %copy-start.13 = (s32[16,16]{1,0:T(8,128)S(1)}, s32[16,16]{1,0:T(8,128)}, u32[]{:S(2)}) copy-start(s32[16,16]{1,0:T(8,128)} %orient_ref.3) | copy-start | bytes 3076
  0.8 30.0 %copy-start.12 = (s32[16,16]{1,0:T(8,128)S(1)}, s32[16,16]{1,0:T(8,128)}, u32[]{:S(2)}) copy-start(s32[16,16]{1,0:T(8,128)} %inst_ref.3) | copy-start | bytes 3076
  0.8 30.0 %copy-start.16 = (f32[8]{0:T(128)S(1)}, f32[8]{0:T(128)}, u32[]{:S(2)}) copy-start(f32[8]{0:T(128)} %weights_ref.1) | copy-start | bytes 100
  30.8 29.8 %copy-start.1 = (bf16[128,512]{1,0:T(8,128)(2,1)S(1)}, bf16[128,512]{1,0:T(8,128)(2,1)}, u32[]{:S(2)}) copy-start(bf16[128,512]{1,0:T(8,128)(2,1)} %constant.35.clone.spread_hbm.spread_ref) | copy-start | bytes 393220
  30.8 29.8 %copy-start.14 = (f32[2,64,128]{2,1,0:T(8,128)S(1)}, f32[2,64,128]{2,1,0:T(8,128)}, u32[]{:S(2)}) copy-start(f32[2,64,128]{2,1,0:T(8,128)} %get-tuple-element.13.own_ref) | copy-start | bytes 196612
